TPU v7x, 256 devices: a whole 4x4x8 slice. The times are simulated.
256 devices in a mesh: section: 8 (over y_hi, x), dp: 32 (over z, y_lo, core).
Axes of the slice: x: 4, y: 4 (y_hi: 2, y_lo: 2; y = y_hi * 2 + y_lo), z: 8, core: 2. Of those that a mesh axis runs over, the one named last changes fastest.
Arguments:
- tokens: bfloat16 [15360, 2048], P('dp'), may hold values from -6 to 6
- cotangent: bfloat16 [15360, 2048], P('dp'), may hold values from -6 to 6
- w_gate: bfloat16 [8, 2048, 512], P('section'), may hold values from -0.125 to 0.125
- w_up: bfloat16 [8, 2048, 512], P('section'), may hold values from -0.125 to 0.125
- w_down: bfloat16 [8, 2048, 512], P('section'), may hold values from -0.25 to 0.25
Outputs:
- input_grad: bfloat16 [8, 15360, 2048], P('section', 'dp')
- grad_gate: float32 [8, 2048, 512], P('section', 'dp')
- grad_up: float32 [8, 2048, 512], P('section', 'dp')
- grad_down: float32 [8, 2048, 512], P('section', 'dp')
All inputs are finite; a program needn't handle non-finite values.
Results may differ from a plain program's by a relative error of at most 0.035.
Values may be sent and summed in bfloat16 or wider, within the bound.
A program may use at most 128 MiB of HBM per device.

v0:
```python
import jax
import jax.numpy as jnp
from jax import lax
from jax.sharding import Mesh
from jax.sharding import PartitionSpec as P

MICRO = 3
DP = ("dp_0", "dp_1", "dp_2")


def passed_along(block, axis, distance):
    devices = range(lax.axis_size(axis))
    route = [(i - distance, i) for i in devices if i - distance in devices]
    return lax.ppermute(block, axis, route)


def reduced_to_own(blocks, axes, sequence):
    inside = blocks.shape[1:]
    blocks = blocks.reshape(*(lax.axis_size(a) for a in axes), *inside)
    blocks = jnp.moveaxis(blocks, sequence, range(len(axes))).reshape(-1, *inside)
    for k in sequence:
        blocks = lax.psum_scatter(blocks, axes[k], scatter_dimension=0, tiled=True)
    return blocks[0]


def split_up(array, dim, count):
    before, after = (array.shape[:dim], array.shape[dim + 1 :])
    return jnp.moveaxis(array.reshape(*before, count, -1, *after), dim, 0)


def summed_rows_2(array, axes, sequence, dim):
    count = lax.axis_size(axes)
    return reduced_to_own(split_up(array, dim, count), axes, sequence)


def forward_layer(layer_input_rows, w_gate, w_up, w_down):
    xf = layer_input_rows.astype(jnp.float32)
    inverse_norm_scale = lax.rsqrt(jnp.mean(xf * xf, axis=-1, keepdims=True) + 1e-06)
    normed = (xf * inverse_norm_scale).astype(jnp.bfloat16)
    gate = jnp.dot(normed, w_gate, preferred_element_type=jnp.float32)
    upper = jnp.dot(normed, w_up, preferred_element_type=jnp.float32)
    hidden = (gate * jax.nn.sigmoid(gate) * upper).astype(jnp.bfloat16)
    branch = lax.dot_general(
        hidden, w_down, (((1,), (1,)), ((), ())), preferred_element_type=jnp.float32
    )
    return ((xf + branch).astype(jnp.bfloat16), normed, inverse_norm_scale, gate, upper, hidden)


def backward_layer(
    layer_input_rows, arriving_gradient, inverse_norm_scale, gate, upper, w_gate, w_up, w_down
):
    d_hidden = jnp.dot(arriving_gradient, w_down, preferred_element_type=jnp.float32)
    sig = jax.nn.sigmoid(gate)
    d_gate = (d_hidden * upper * sig * (1.0 + gate * (1.0 - sig))).astype(jnp.bfloat16)
    d_upper = (d_hidden * gate * sig).astype(jnp.bfloat16)
    dims = (((1,), (1,)), ((), ()))
    normalized_gradient = lax.dot_general(d_gate, w_gate, dims, preferred_element_type=jnp.float32)
    normalized_gradient = normalized_gradient + lax.dot_general(
        d_upper, w_up, dims, preferred_element_type=jnp.float32
    )
    normalized_input = layer_input_rows.astype(jnp.float32) * inverse_norm_scale
    inner_product_sum = jnp.mean(normalized_gradient * normalized_input, axis=-1, keepdims=True)
    input_gradient_rows = (
        arriving_gradient.astype(jnp.float32)
        + inverse_norm_scale * (normalized_gradient - normalized_input * inner_product_sum)
    ).astype(jnp.bfloat16)
    return (input_gradient_rows, d_gate, d_upper)


def store_slot(buffer, value, index, valid):
    previous = lax.dynamic_index_in_dim(buffer, index, 0, keepdims=False)
    chosen = jnp.where(valid, value, previous)
    return lax.dynamic_update_index_in_dim(buffer, chosen, index, 0)


def send_back(input_gradient_rows):
    return passed_along(input_gradient_rows, "section", -1)


def body(tokens, cotangent, w_gate, w_up, w_down):
    sections = lax.axis_size("section")
    place = lax.axis_index("section")
    micro = MICRO
    tok_rows = tokens.shape[0]
    rows = tok_rows // micro
    width = tokens.shape[1]
    gate_w = w_gate[0]
    up_w = w_up[0]
    down_w = w_down[0]
    units = gate_w.shape[1]
    ticks = sections + micro - 1
    rows_dims = (((0,), (0,)), ((), ()))
    batches = tokens.reshape(micro, rows, width)
    cot_batches = cotangent.reshape(micro, rows, width)
    zero_act = jnp.zeros((rows, width), jnp.bfloat16)
    zero_units = jnp.zeros((rows, units), jnp.float32)

    def forward_tick(tick, carry):
        arrived, saved, kept_gate, kept_up = carry
        slot = tick - place
        valid = (slot >= 0) & (slot < micro)
        index = jnp.clip(slot, 0, micro - 1)
        first = lax.dynamic_index_in_dim(batches, index, 0, keepdims=False)
        entry = jnp.where(place == 0, first, arrived)

        def forward_work(operand):
            result, normed, inverse_norm_scale, gate, upper, hidden = forward_layer(
                operand, gate_w, up_w, down_w
            )
            return (result, gate, upper)

        def forward_skip(operand):
            return (zero_act, zero_units, zero_units)

        result, gate, upper = lax.cond(valid, forward_work, forward_skip, entry)
        saved = store_slot(saved, entry, index, valid)
        kept_gate = store_slot(kept_gate, gate, index, valid)
        kept_up = store_slot(kept_up, upper, index, valid)
        arrived = passed_along(result, "section", 1)
        return (arrived, saved, kept_gate, kept_up)

    keep_shape = (micro, rows, units)
    start = (
        zero_act,
        jnp.zeros((micro, rows, width), jnp.bfloat16),
        jnp.zeros(keep_shape, jnp.float32),
        jnp.zeros(keep_shape, jnp.float32),
    )
    _, saved, kept_gate, kept_up = lax.fori_loop(0, ticks, forward_tick, start)

    def backward_parts(layer_input_rows, arriving_gradient, index):
        xf = layer_input_rows.astype(jnp.float32)
        inverse_norm_scale = lax.rsqrt(jnp.mean(xf * xf, axis=-1, keepdims=True) + 1e-06)
        normed = (xf * inverse_norm_scale).astype(jnp.bfloat16)
        gate = lax.dynamic_index_in_dim(kept_gate, index, 0, keepdims=False)
        upper = lax.dynamic_index_in_dim(kept_up, index, 0, keepdims=False)
        hidden = (gate * jax.nn.sigmoid(gate) * upper).astype(jnp.bfloat16)
        input_gradient_rows, d_gate, d_upper = backward_layer(
            layer_input_rows,
            arriving_gradient,
            inverse_norm_scale,
            gate,
            upper,
            gate_w,
            up_w,
            down_w,
        )
        return (input_gradient_rows, normed, d_gate, d_upper, hidden)

    def backward_tick(tick, carry):
        arrived, grads_in, st_norm, st_gate, st_up, st_hidden, st_cot = carry
        slot = tick - (sections - 1 - place)
        valid = (slot >= 0) & (slot < micro)
        index = jnp.clip(slot, 0, micro - 1)
        last = lax.dynamic_index_in_dim(cot_batches, index, 0, keepdims=False)
        arriving_gradient = jnp.where(place == sections - 1, last, arrived)
        layer_input_rows = lax.dynamic_index_in_dim(saved, index, 0, keepdims=False)

        def backward_work(operands):
            return backward_parts(operands[0], operands[1], index)

        def backward_skip(operands):
            zeros_narrow = jnp.zeros((rows, units), jnp.bfloat16)
            return (zero_act, zero_act, zeros_narrow, zeros_narrow, zeros_narrow)

        input_gradient_rows, normed, d_gate, d_upper, hidden = lax.cond(
            valid, backward_work, backward_skip, (layer_input_rows, arriving_gradient)
        )
        grads_in = store_slot(grads_in, input_gradient_rows, index, valid)
        st_norm = store_slot(st_norm, normed, index, valid)
        st_gate = store_slot(st_gate, d_gate, index, valid)
        st_up = store_slot(st_up, d_upper, index, valid)
        st_hidden = store_slot(st_hidden, hidden, index, valid)
        st_cot = store_slot(st_cot, arriving_gradient, index, valid)
        arrived = send_back(input_gradient_rows)
        return (arrived, grads_in, st_norm, st_gate, st_up, st_hidden, st_cot)

    wide = jnp.zeros((micro, rows, width), jnp.bfloat16)
    narrow = jnp.zeros((micro, rows, units), jnp.bfloat16)
    start = (zero_act, wide, wide, narrow, narrow, narrow, wide)
    _, grads_in, st_norm, st_gate, st_up, st_hidden, st_cot = lax.fori_loop(
        0, ticks, backward_tick, start
    )
    all_norm = st_norm.reshape(tok_rows, width)
    all_cot = st_cot.reshape(tok_rows, width)
    all_gate = st_gate.reshape(tok_rows, units)
    all_up = st_up.reshape(tok_rows, units)
    all_hidden = st_hidden.reshape(tok_rows, units)
    part_g = lax.dot_general(all_norm, all_gate, rows_dims, preferred_element_type=jnp.float32)
    part_u = lax.dot_general(all_norm, all_up, rows_dims, preferred_element_type=jnp.float32)
    part_d = lax.dot_general(all_cot, all_hidden, rows_dims, preferred_element_type=jnp.float32)
    summed = summed_rows_2(
        jnp.concatenate([part_g, part_u, part_d], axis=1).astype(jnp.bfloat16), DP, (2, 0, 1), 0
    ).astype(jnp.float32)
    grad_g = summed[:, :units]
    grad_u = summed[:, units : 2 * units]
    grad_d = summed[:, 2 * units :]
    return (grads_in.reshape(1, tok_rows, width), grad_g[None], grad_u[None], grad_d[None])


def solution(mesh):
    torus = Mesh(
        mesh.devices.reshape(mesh.shape["section"], 8, 2, 2), ("section", "dp_0", "dp_1", "dp_2")
    )
    placed = (
        P(DP, None),
        P(DP, None),
        P("section", None, None),
        P("section", None, None),
        P("section", None, None),
    )
    return jax.shard_map(
        body,
        mesh=torus,
        in_specs=placed,
        out_specs=(
            P("section", DP, None),
            P("section", DP, None),
            P("section", DP, None),
            P("section", DP, None),
        ),
        check_vma=False,
    )
```

profile of v0, /device:TPU:8, one launch (start us, length us, event | category | flops | bytes accessed | tf_op | source)
XLA Modules:
  0.0 630.4 jit_solution(1341867753736919712)
XLA Ops:
  11.0 228.0 %while.47 = (s32[]{:T(128)}, bf16[160,2048]{1,0:T(8,128)(2,1)S(1)}, bf16[3,160,2048]{2,1,0:T(8,128)(2,1)}, f32[3,160,512]{2,1,0:T(8,128)}, f32[3,160,512]{2,1,0:...) while((s32[]{:T(128)}, bf16[160,2048]{1,0:T(8,128)(2,1)S(1)}, ...), condition=%wide.region_4.5_spmd, body=%wide.region_0.4_spmd.sunk | while | flops 1011875968 | bytes 38146040 | solution.py:129
  24.9 10.2 %collective-permute-done = bf16[160,2048]{1,0:T(8,128)(2,1)S(1)} collective-permute-done((bf16[160,2048]{1,0:T(8,128)(2,1)S(1)}, bf16[160,2048]{1,0:T(8,128)(2,1)S(1)}, u32[]{:S(2)}, u32[]{:S(2)}) %collective-permute-start) | collective-permute-done | bytes 655392 | tf_op jit(solution)/shard_map/while/body/eval_jaxpr/ppermute | solution.py:14
  52.0 9.3 %collective-permute-done = bf16[160,2048]{1,0:T(8,128)(2,1)S(1)} collective-permute-done((bf16[160,2048]{1,0:T(8,128)(2,1)S(1)}, bf16[160,2048]{1,0:T(8,128)(2,1)S(1)}, u32[]{:S(2)}, u32[]{:S(2)}) %collective-permute-start) | collective-permute-done | bytes 655392 | tf_op jit(solution)/shard_map/while/body/eval_jaxpr/ppermute | solution.py:14
  78.2 8.4 %collective-permute-done = bf16[160,2048]{1,0:T(8,128)(2,1)S(1)} collective-permute-done((bf16[160,2048]{1,0:T(8,128)(2,1)S(1)}, bf16[160,2048]{1,0:T(8,128)(2,1)S(1)}, u32[]{:S(2)}, u32[]{:S(2)}) %collective-permute-start) | collective-permute-done | bytes 655392 | tf_op jit(solution)/shard_map/while/body/eval_jaxpr/ppermute | solution.py:14
  92.0 7.6 %collective-permute-start = (bf16[160,2048]{1,0:T(8,128)(2,1)S(1)}, bf16[160,2048]{1,0:T(8,128)(2,1)S(1)}, u32[]{:S(2)}, u32[]{:S(2)}) collective-permute-start(bf16[160,2048]{1,0:T(8,128)(2,1)S(1)} %get-tuple-element.929), channel_id=1, source_target_pairs={{0,32},{32,64},{64,96},{96,128},{128,160},{160,192},{192,224},{1,3... | collective-permute-start | bytes 1966088 | tf_op jit(solution)/shard_map/while/body/eval_jaxpr/ppermute | solution.py:14
  102.5 8.5 %collective-permute-done = bf16[160,2048]{1,0:T(8,128)(2,1)S(1)} collective-permute-done((bf16[160,2048]{1,0:T(8,128)(2,1)S(1)}, bf16[160,2048]{1,0:T(8,128)(2,1)S(1)}, u32[]{:S(2)}, u32[]{:S(2)}) %collective-permute-start) | collective-permute-done | bytes 655392 | tf_op jit(solution)/shard_map/while/body/eval_jaxpr/ppermute | solution.py:14
  123.8 7.6 %collective-permute-done = bf16[160,2048]{1,0:T(8,128)(2,1)S(1)} collective-permute-done((bf16[160,2048]{1,0:T(8,128)(2,1)S(1)}, bf16[160,2048]{1,0:T(8,128)(2,1)S(1)}, u32[]{:S(2)}, u32[]{:S(2)}) %collective-permute-start) | collective-permute-done | bytes 655392 | tf_op jit(solution)/shard_map/while/body/eval_jaxpr/ppermute | solution.py:14
  136.7 6.2 collective-permute-start
  145.9 6.9 %collective-permute-done = bf16[160,2048]{1,0:T(8,128)(2,1)S(1)} collective-permute-done((bf16[160,2048]{1,0:T(8,128)(2,1)S(1)}, bf16[160,2048]{1,0:T(8,128)(2,1)S(1)}, u32[]{:S(2)}, u32[]{:S(2)}) %collective-permute-start) | collective-permute-done | bytes 655392 | tf_op jit(solution)/shard_map/while/body/eval_jaxpr/ppermute | solution.py:14
  165.7 6.0 collective-permute-done
  177.1 7.9 %collective-permute-start = (bf16[160,2048]{1,0:T(8,128)(2,1)S(1)}, bf16[160,2048]{1,0:T(8,128)(2,1)S(1)}, u32[]{:S(2)}, u32[]{:S(2)}) collective-permute-start(bf16[160,2048]{1,0:T(8,128)(2,1)S(1)} %get-tuple-element.929), channel_id=1, source_target_pairs={{0,32},{32,64},{64,96},{96,128},{128,160},{160,192},{192,224},{1,3... | collective-permute-start | bytes 1966088 | tf_op jit(solution)/shard_map/while/body/eval_jaxpr/ppermute | solution.py:14
  188.0 5.1 collective-permute-done
  198.4 8.0 %collective-permute-start = (bf16[160,2048]{1,0:T(8,128)(2,1)S(1)}, bf16[160,2048]{1,0:T(8,128)(2,1)S(1)}, u32[]{:S(2)}, u32[]{:S(2)}) collective-permute-start(bf16[160,2048]{1,0:T(8,128)(2,1)S(1)} %get-tuple-element.929), channel_id=1, source_target_pairs={{0,32},{32,64},{64,96},{96,128},{128,160},{160,192},{192,224},{1,3... | collective-permute-start | bytes 1966088 | tf_op jit(solution)/shard_map/while/body/eval_jaxpr/ppermute | solution.py:14
  209.4 5.1 collective-permute-done
  219.8 11.2 %collective-permute-start = (bf16[160,2048]{1,0:T(8,128)(2,1)S(1)}, bf16[160,2048]{1,0:T(8,128)(2,1)S(1)}, u32[]{:S(2)}, u32[]{:S(2)}) collective-permute-start(bf16[160,2048]{1,0:T(8,128)(2,1)S(1)} %get-tuple-element.929), channel_id=1, source_target_pairs={{0,32},{32,64},{64,96},{96,128},{128,160},{160,192},{192,224},{1,3... | collective-permute-start | bytes 1966088 | tf_op jit(solution)/shard_map/while/body/eval_jaxpr/ppermute | solution.py:14
  234.0 5.1 collective-permute-done
  247.1 263.9 %while.48 = (s32[]{:T(128)}, bf16[160,2048]{1,0:T(8,128)(2,1)}, bf16[3,160,2048]{2,1,0:T(8,128)(2,1)}, bf16[3,160,2048]{2,1,0:T(8,128)(2,1)}, bf16[3,160,512]{2,...) while((s32[]{:T(128)}, bf16[160,2048]{1,0:T(8,128)(2,1)}, ...), condition=%wide.region_10.11_spmd, body=%wide.region_5.10_spmd.sunk | while | flops 1015070848 | bytes 52699816 | solution.py:181
  263.3 7.4 %collective-permute-done.1 = bf16[160,2048]{1,0:T(8,128)(2,1)} collective-permute-done((bf16[160,2048]{1,0:T(8,128)(2,1)}, bf16[160,2048]{1,0:T(8,128)(2,1)}, u32[]{:S(2)}, u32[]{:S(2)}) %collective-permute-start.1) | collective-permute-done | bytes 655392 | tf_op jit(solution)/shard_map/while/body/eval_jaxpr/ppermute | solution.py:14
  286.9 7.4 %collective-permute-done.1 = bf16[160,2048]{1,0:T(8,128)(2,1)} collective-permute-done((bf16[160,2048]{1,0:T(8,128)(2,1)}, bf16[160,2048]{1,0:T(8,128)(2,1)}, u32[]{:S(2)}, u32[]{:S(2)}) %collective-permute-start.1) | collective-permute-done | bytes 655392 | tf_op jit(solution)/shard_map/while/body/eval_jaxpr/ppermute | solution.py:14
  310.5 7.4 %collective-permute-done.1 = bf16[160,2048]{1,0:T(8,128)(2,1)} collective-permute-done((bf16[160,2048]{1,0:T(8,128)(2,1)}, bf16[160,2048]{1,0:T(8,128)(2,1)}, u32[]{:S(2)}, u32[]{:S(2)}) %collective-permute-start.1) | collective-permute-done | bytes 655392 | tf_op jit(solution)/shard_map/while/body/eval_jaxpr/ppermute | solution.py:14
  334.0 7.4 %collective-permute-done.1 = bf16[160,2048]{1,0:T(8,128)(2,1)} collective-permute-done((bf16[160,2048]{1,0:T(8,128)(2,1)}, bf16[160,2048]{1,0:T(8,128)(2,1)}, u32[]{:S(2)}, u32[]{:S(2)}) %collective-permute-start.1) | collective-permute-done | bytes 655392 | tf_op jit(solution)/shard_map/while/body/eval_jaxpr/ppermute | solution.py:14
  357.6 6.9 %collective-permute-done.1 = bf16[160,2048]{1,0:T(8,128)(2,1)} collective-permute-done((bf16[160,2048]{1,0:T(8,128)(2,1)}, bf16[160,2048]{1,0:T(8,128)(2,1)}, u32[]{:S(2)}, u32[]{:S(2)}) %collective-permute-start.1) | collective-permute-done | bytes 655392 | tf_op jit(solution)/shard_map/while/body/eval_jaxpr/ppermute | solution.py:14
  380.7 6.9 %collective-permute-done.1 = bf16[160,2048]{1,0:T(8,128)(2,1)} collective-permute-done((bf16[160,2048]{1,0:T(8,128)(2,1)}, bf16[160,2048]{1,0:T(8,128)(2,1)}, u32[]{:S(2)}, u32[]{:S(2)}) %collective-permute-start.1) | collective-permute-done | bytes 655392 | tf_op jit(solution)/shard_map/while/body/eval_jaxpr/ppermute | solution.py:14
  403.8 23.3 %collective-permute-done.1 = bf16[160,2048]{1,0:T(8,128)(2,1)} collective-permute-done((bf16[160,2048]{1,0:T(8,128)(2,1)}, bf16[160,2048]{1,0:T(8,128)(2,1)}, u32[]{:S(2)}, u32[]{:S(2)}) %collective-permute-start.1) | collective-permute-done | bytes 655392 | tf_op jit(solution)/shard_map/while/body/eval_jaxpr/ppermute | solution.py:14
  430.8 8.5 %conditional.5 = (bf16[160,2048]{1,0:T(8,128)(2,1)}, bf16[160,2048]{1,0:T(8,128)(2,1)S(1)}, bf16[160,512]{1,0:T(8,128)(2,1)}, bf16[160,512]{1,0:T(8,128)(2,1)}, bf16[160,512]{1,0:T(8,128)(2,1)}) conditional(s32[]{:T(128)} %convert_element_type.104, () %tuple.114, (bf16[160,2048]{1,0:T(8,128)(2,1)S(1)}, bf16[3,160,2048]{2,1,0:T(8,128)(2,1)}, ...), branch_computations={%region_6.6_spmd, %region_7.9_spmd} | conditional | flops 1013514368 | bytes 33855248 | solution.py:166
  459.4 8.5 %conditional.5 = (bf16[160,2048]{1,0:T(8,128)(2,1)}, bf16[160,2048]{1,0:T(8,128)(2,1)S(1)}, bf16[160,512]{1,0:T(8,128)(2,1)}, bf16[160,512]{1,0:T(8,128)(2,1)}, bf16[160,512]{1,0:T(8,128)(2,1)}) conditional(s32[]{:T(128)} %convert_element_type.104, () %tuple.114, (bf16[160,2048]{1,0:T(8,128)(2,1)S(1)}, bf16[3,160,2048]{2,1,0:T(8,128)(2,1)}, ...), branch_computations={%region_6.6_spmd, %region_7.9_spmd} | conditional | flops 1013514368 | bytes 33855248 | solution.py:166
  480.5 5.5 collective-permute-done.1
  489.7 8.5 %conditional.5 = (bf16[160,2048]{1,0:T(8,128)(2,1)}, bf16[160,2048]{1,0:T(8,128)(2,1)S(1)}, bf16[160,512]{1,0:T(8,128)(2,1)}, bf16[160,512]{1,0:T(8,128)(2,1)}, bf16[160,512]{1,0:T(8,128)(2,1)}) conditional(s32[]{:T(128)} %convert_element_type.104, () %tuple.114, (bf16[160,2048]{1,0:T(8,128)(2,1)S(1)}, bf16[3,160,2048]{2,1,0:T(8,128)(2,1)}, ...), branch_computations={%region_6.6_spmd, %region_7.9_spmd} | conditional | flops 1013514368 | bytes 33855248 | solution.py:166
  517.0 4.7 maximum_bitcast_fusion
  525.2 27.0 %reduce-scatter.4.cloned.1.call-done = bf16[16,64,1536]{2,1,0:T(8,128)(2,1)} async-done(((bf16[32,64,1536]{2,1,0:T(8,128)(2,1)}), bf16[16,64,1536]{2,1,0:T(8,128)(2,1)}) %reduce-scatter.4.cloned.1.call-update) | async-done | bytes 3145744 | tf_op jit(solution)/shard_map/reduce_scatter | solution.py:22
  552.3 50.6 %reduce-scatter.6.cloned.1.call-done = bf16[2,64,1536]{2,1,0:T(8,128)(2,1)} async-done(((bf16[16,64,1536]{2,1,0:T(8,128)(2,1)}), bf16[2,64,1536]{2,1,0:T(8,128)(2,1)}) %reduce-scatter.6.cloned.1.call-update) | async-done | bytes 393232 | tf_op jit(solution)/shard_map/reduce_scatter | solution.py:22
  602.9 19.3 %reduce-scatter.8.cloned.1.call-done = bf16[1,64,1536]{2,1,0:T(8,128)(2,1)} async-done(((bf16[2,64,1536]{2,1,0:T(8,128)(2,1)}), bf16[1,64,1536]{2,1,0:T(8,128)(2,1)}) %reduce-scatter.8.cloned.1.call-update) | async-done | bytes 196624 | tf_op jit(solution)/shard_map/reduce_scatter | solution.py:22
  (381 shorter events, 375.2 us)
Async XLA Ops:
  7.2 545.0 %reduce-scatter.4.cloned.1.call-start = ((), (), s32[]{:S(2)}) async-start(), calls=%async_computation.3 | async-start | bytes 9437184 | tf_op jit(solution)/shard_map/reduce_scatter | solution.py:22
  19.5 15.5 %collective-permute-start = (bf16[160,2048]{1,0:T(8,128)(2,1)S(1)}, bf16[160,2048]{1,0:T(8,128)(2,1)S(1)}, u32[]{:S(2)}, u32[]{:S(2)}) collective-permute-start(bf16[160,2048]{1,0:T(8,128)(2,1)S(1)} %get-tuple-element.929), channel_id=1, source_target_pairs={{0,32},{32,64},{64,96},{96,128},{128,160},{160,192},{192,224},{1,3... | collective-permute-start | bytes 1966088 | tf_op jit(solution)/shard_map/while/body/eval_jaxpr/ppermute | solution.py:14
  43.5 17.8 %collective-permute-start = (bf16[160,2048]{1,0:T(8,128)(2,1)S(1)}, bf16[160,2048]{1,0:T(8,128)(2,1)S(1)}, u32[]{:S(2)}, u32[]{:S(2)}) collective-permute-start(bf16[160,2048]{1,0:T(8,128)(2,1)S(1)} %get-tuple-element.929), channel_id=1, source_target_pairs={{0,32},{32,64},{64,96},{96,128},{128,160},{160,192},{192,224},{1,3... | collective-permute-start | bytes 1966088 | tf_op jit(solution)/shard_map/while/body/eval_jaxpr/ppermute | solution.py:14
  69.8 16.8 %collective-permute-start = (bf16[160,2048]{1,0:T(8,128)(2,1)S(1)}, bf16[160,2048]{1,0:T(8,128)(2,1)S(1)}, u32[]{:S(2)}, u32[]{:S(2)}) collective-permute-start(bf16[160,2048]{1,0:T(8,128)(2,1)S(1)} %get-tuple-element.929), channel_id=1, source_target_pairs={{0,32},{32,64},{64,96},{96,128},{128,160},{160,192},{192,224},{1,3... | collective-permute-start | bytes 1966088 | tf_op jit(solution)/shard_map/while/body/eval_jaxpr/ppermute | solution.py:14
  92.0 19.0 %collective-permute-start = (bf16[160,2048]{1,0:T(8,128)(2,1)S(1)}, bf16[160,2048]{1,0:T(8,128)(2,1)S(1)}, u32[]{:S(2)}, u32[]{:S(2)}) collective-permute-start(bf16[160,2048]{1,0:T(8,128)(2,1)S(1)} %get-tuple-element.929), channel_id=1, source_target_pairs={{0,32},{32,64},{64,96},{96,128},{128,160},{160,192},{192,224},{1,3... | collective-permute-start | bytes 1966088 | tf_op jit(solution)/shard_map/while/body/eval_jaxpr/ppermute | solution.py:14
  116.4 15.0 %collective-permute-start = (bf16[160,2048]{1,0:T(8,128)(2,1)S(1)}, bf16[160,2048]{1,0:T(8,128)(2,1)S(1)}, u32[]{:S(2)}, u32[]{:S(2)}) collective-permute-start(bf16[160,2048]{1,0:T(8,128)(2,1)S(1)} %get-tuple-element.929), channel_id=1, source_target_pairs={{0,32},{32,64},{64,96},{96,128},{128,160},{160,192},{192,224},{1,3... | collective-permute-start | bytes 1966088 | tf_op jit(solution)/shard_map/while/body/eval_jaxpr/ppermute | solution.py:14
  136.7 16.2 %collective-permute-start = (bf16[160,2048]{1,0:T(8,128)(2,1)S(1)}, bf16[160,2048]{1,0:T(8,128)(2,1)S(1)}, u32[]{:S(2)}, u32[]{:S(2)}) collective-permute-start(bf16[160,2048]{1,0:T(8,128)(2,1)S(1)} %get-tuple-element.929), channel_id=1, source_target_pairs={{0,32},{32,64},{64,96},{96,128},{128,160},{160,192},{192,224},{1,3... | collective-permute-start | bytes 1966088 | tf_op jit(solution)/shard_map/while/body/eval_jaxpr/ppermute | solution.py:14
  158.3 13.4 %collective-permute-start = (bf16[160,2048]{1,0:T(8,128)(2,1)S(1)}, bf16[160,2048]{1,0:T(8,128)(2,1)S(1)}, u32[]{:S(2)}, u32[]{:S(2)}) collective-permute-start(bf16[160,2048]{1,0:T(8,128)(2,1)S(1)} %get-tuple-element.929), channel_id=1, source_target_pairs={{0,32},{32,64},{64,96},{96,128},{128,160},{160,192},{192,224},{1,3... | collective-permute-start | bytes 1966088 | tf_op jit(solution)/shard_map/while/body/eval_jaxpr/ppermute | solution.py:14
  177.1 16.0 %collective-permute-start = (bf16[160,2048]{1,0:T(8,128)(2,1)S(1)}, bf16[160,2048]{1,0:T(8,128)(2,1)S(1)}, u32[]{:S(2)}, u32[]{:S(2)}) collective-permute-start(bf16[160,2048]{1,0:T(8,128)(2,1)S(1)} %get-tuple-element.929), channel_id=1, source_target_pairs={{0,32},{32,64},{64,96},{96,128},{128,160},{160,192},{192,224},{1,3... | collective-permute-start | bytes 1966088 | tf_op jit(solution)/shard_map/while/body/eval_jaxpr/ppermute | solution.py:14
  198.4 16.0 %collective-permute-start = (bf16[160,2048]{1,0:T(8,128)(2,1)S(1)}, bf16[160,2048]{1,0:T(8,128)(2,1)S(1)}, u32[]{:S(2)}, u32[]{:S(2)}) collective-permute-start(bf16[160,2048]{1,0:T(8,128)(2,1)S(1)} %get-tuple-element.929), channel_id=1, source_target_pairs={{0,32},{32,64},{64,96},{96,128},{128,160},{160,192},{192,224},{1,3... | collective-permute-start | bytes 1966088 | tf_op jit(solution)/shard_map/while/body/eval_jaxpr/ppermute | solution.py:14
  219.8 19.2 %collective-permute-start = (bf16[160,2048]{1,0:T(8,128)(2,1)S(1)}, bf16[160,2048]{1,0:T(8,128)(2,1)S(1)}, u32[]{:S(2)}, u32[]{:S(2)}) collective-permute-start(bf16[160,2048]{1,0:T(8,128)(2,1)S(1)} %get-tuple-element.929), channel_id=1, source_target_pairs={{0,32},{32,64},{64,96},{96,128},{128,160},{160,192},{192,224},{1,3... | collective-permute-start | bytes 1966088 | tf_op jit(solution)/shard_map/while/body/eval_jaxpr/ppermute | solution.py:14
  253.8 4.1 copy-start.4
  253.8 16.9 %collective-permute-start.1 = (bf16[160,2048]{1,0:T(8,128)(2,1)}, bf16[160,2048]{1,0:T(8,128)(2,1)}, u32[]{:S(2)}, u32[]{:S(2)}) collective-permute-start(bf16[160,2048]{1,0:T(8,128)(2,1)} %get-tuple-element.953), channel_id=1, source_target_pairs={{32,0},{64,32},{96,64},{128,96},{160,128},{192,160},{224,192},{33,... | collective-permute-start | bytes 1966088 | tf_op jit(solution)/shard_map/while/body/eval_jaxpr/ppermute | solution.py:14
  277.4 4.1 copy-start.4
  277.4 16.9 %collective-permute-start.1 = (bf16[160,2048]{1,0:T(8,128)(2,1)}, bf16[160,2048]{1,0:T(8,128)(2,1)}, u32[]{:S(2)}, u32[]{:S(2)}) collective-permute-start(bf16[160,2048]{1,0:T(8,128)(2,1)} %get-tuple-element.953), channel_id=1, source_target_pairs={{32,0},{64,32},{96,64},{128,96},{160,128},{192,160},{224,192},{33,... | collective-permute-start | bytes 1966088 | tf_op jit(solution)/shard_map/while/body/eval_jaxpr/ppermute | solution.py:14
  301.0 4.1 copy-start.4
  301.0 16.9 %collective-permute-start.1 = (bf16[160,2048]{1,0:T(8,128)(2,1)}, bf16[160,2048]{1,0:T(8,128)(2,1)}, u32[]{:S(2)}, u32[]{:S(2)}) collective-permute-start(bf16[160,2048]{1,0:T(8,128)(2,1)} %get-tuple-element.953), channel_id=1, source_target_pairs={{32,0},{64,32},{96,64},{128,96},{160,128},{192,160},{224,192},{33,... | collective-permute-start | bytes 1966088 | tf_op jit(solution)/shard_map/while/body/eval_jaxpr/ppermute | solution.py:14
  324.6 4.1 copy-start.4
  324.6 16.9 %collective-permute-start.1 = (bf16[160,2048]{1,0:T(8,128)(2,1)}, bf16[160,2048]{1,0:T(8,128)(2,1)}, u32[]{:S(2)}, u32[]{:S(2)}) collective-permute-start(bf16[160,2048]{1,0:T(8,128)(2,1)} %get-tuple-element.953), channel_id=1, source_target_pairs={{32,0},{64,32},{96,64},{128,96},{160,128},{192,160},{224,192},{33,... | collective-permute-start | bytes 1966088 | tf_op jit(solution)/shard_map/while/body/eval_jaxpr/ppermute | solution.py:14
  348.1 4.1 copy-start.4
  348.1 16.4 %collective-permute-start.1 = (bf16[160,2048]{1,0:T(8,128)(2,1)}, bf16[160,2048]{1,0:T(8,128)(2,1)}, u32[]{:S(2)}, u32[]{:S(2)}) collective-permute-start(bf16[160,2048]{1,0:T(8,128)(2,1)} %get-tuple-element.953), channel_id=1, source_target_pairs={{32,0},{64,32},{96,64},{128,96},{160,128},{192,160},{224,192},{33,... | collective-permute-start | bytes 1966088 | tf_op jit(solution)/shard_map/while/body/eval_jaxpr/ppermute | solution.py:14
  371.3 4.1 copy-start.4
  371.3 16.4 %collective-permute-start.1 = (bf16[160,2048]{1,0:T(8,128)(2,1)}, bf16[160,2048]{1,0:T(8,128)(2,1)}, u32[]{:S(2)}, u32[]{:S(2)}) collective-permute-start(bf16[160,2048]{1,0:T(8,128)(2,1)} %get-tuple-element.953), channel_id=1, source_target_pairs={{32,0},{64,32},{96,64},{128,96},{160,128},{192,160},{224,192},{33,... | collective-permute-start | bytes 1966088 | tf_op jit(solution)/shard_map/while/body/eval_jaxpr/ppermute | solution.py:14
  394.4 4.1 copy-start.4
  394.4 32.8 %collective-permute-start.1 = (bf16[160,2048]{1,0:T(8,128)(2,1)}, bf16[160,2048]{1,0:T(8,128)(2,1)}, u32[]{:S(2)}, u32[]{:S(2)}) collective-permute-start(bf16[160,2048]{1,0:T(8,128)(2,1)} %get-tuple-element.953), channel_id=1, source_target_pairs={{32,0},{64,32},{96,64},{128,96},{160,128},{192,160},{224,192},{33,... | collective-permute-start | bytes 1966088 | tf_op jit(solution)/shard_map/while/body/eval_jaxpr/ppermute | solution.py:14
  439.3 4.1 copy-start.4
  439.3 16.4 %collective-permute-start.1 = (bf16[160,2048]{1,0:T(8,128)(2,1)}, bf16[160,2048]{1,0:T(8,128)(2,1)}, u32[]{:S(2)}, u32[]{:S(2)}) collective-permute-start(bf16[160,2048]{1,0:T(8,128)(2,1)} %get-tuple-element.953), channel_id=1, source_target_pairs={{32,0},{64,32},{96,64},{128,96},{160,128},{192,160},{224,192},{33,... | collective-permute-start | bytes 1966088 | tf_op jit(solution)/shard_map/while/body/eval_jaxpr/ppermute | solution.py:14
  467.9 18.2 %collective-permute-start.1 = (bf16[160,2048]{1,0:T(8,128)(2,1)}, bf16[160,2048]{1,0:T(8,128)(2,1)}, u32[]{:S(2)}, u32[]{:S(2)}) collective-permute-start(bf16[160,2048]{1,0:T(8,128)(2,1)} %get-tuple-element.953), channel_id=1, source_target_pairs={{32,0},{64,32},{96,64},{128,96},{160,128},{192,160},{224,192},{33,... | collective-permute-start | bytes 1966088 | tf_op jit(solution)/shard_map/while/body/eval_jaxpr/ppermute | solution.py:14
  498.2 4.1 copy-start.4
  498.2 12.8 %collective-permute-start.1 = (bf16[160,2048]{1,0:T(8,128)(2,1)}, bf16[160,2048]{1,0:T(8,128)(2,1)}, u32[]{:S(2)}, u32[]{:S(2)}) collective-permute-start(bf16[160,2048]{1,0:T(8,128)(2,1)} %get-tuple-element.953), channel_id=1, source_target_pairs={{32,0},{64,32},{96,64},{128,96},{160,128},{192,160},{224,192},{33,... | collective-permute-start | bytes 1966088 | tf_op jit(solution)/shard_map/while/body/eval_jaxpr/ppermute | solution.py:14
  525.1 77.8 %reduce-scatter.6.cloned.1.call-start = ((), (), s32[]{:S(2)}) async-start(), calls=%async_computation.4 | async-start | bytes 3538944 | tf_op jit(solution)/shard_map/reduce_scatter | solution.py:22
  552.2 70.0 %reduce-scatter.8.cloned.1.call-start = ((), (), s32[]{:S(2)}) async-start(), calls=%async_computation.5 | async-start | bytes 589824 | tf_op jit(solution)/shard_map/reduce_scatter | solution.py:22
  (32 other events, 95.4 us)
Sparse Core Ops, SparseCore 0:
  525.3 26.8 reduce-scatter.3
  554.9 47.9 reduce-scatter.5
  605.6 16.5 reduce-scatter.7
where the time goes:
time: 637 us; the launch traced here: 630 us
  waiting for transfers between devices  245 us (38%)
  local copies, waits for them, and re-layouts  144 us (23%)
  other arithmetic  114 us (18%)
  starting transfers between devices  72.8 us (11%)
  matrix products  40 us (6%)
  between operations  13.8 us (2%)
    ppermute x20, waiting for transfers between devices, passed_along(): return lax.ppermute(block, axis, route)  148 us
    dynamic_update_slice x60, other arithmetic, store_slot(): return lax.dynamic_update_index_in_dim(buffer, chosen, index, 0)  103 us
    reduce_scatter x3, waiting for transfers between devices, reduced_to_own(): blocks = lax.psum_scatter(blocks, axes[k], scatter_dimension=0, tiled=True)  96.9 us
    dynamic_slice x90, local copies, waits for them, and re-layouts, store_slot(): previous = lax.dynamic_index_in_dim(buffer, index, 0, keepdims=False)  95 us
    ppermute x20, starting transfers between devices, passed_along(): return lax.ppermute(block, axis, route)  72.7 us
    another operation x27, local copies, waits for them, and re-layouts  22.5 us
  transfers between devices with their start and end apart: 23, of which 23 were waited for; matrix products, arithmetic and copies ran while one was open for 20% of the time, Pallas kernels for 0%

commit v1 on v0

v1 whole, which is shorter than its diff:
```python
import functools

import jax
import jax.numpy as jnp
from jax import lax
from jax.experimental import pallas as pl
from jax.experimental.pallas import tpu as pltpu
from jax.sharding import Mesh
from jax.sharding import PartitionSpec as P

MICRO = 15
AHEAD = 3
CHUNKS = 2
DP = ("dp_0", "dp_1", "dp_2")
MESH = pl.DeviceIdType.MESH
F32 = jnp.float32
BF16 = jnp.bfloat16
ROWS_ROWS = (((0,), (0,)), ((), ()))
LAST_LAST = (((1,), (1,)), ((), ()))


def reduced_to_own(blocks, axes, sequence):
    inside = blocks.shape[1:]
    blocks = blocks.reshape(*(lax.axis_size(a) for a in axes), *inside)
    blocks = jnp.moveaxis(blocks, sequence, range(len(axes))).reshape(-1, *inside)
    for k in sequence:
        blocks = lax.psum_scatter(blocks, axes[k], scatter_dimension=0, tiled=True)
    return blocks[0]


def pipeline_kernel(
    sections,
    micro,
    tok,
    cot,
    wg_h,
    wu_h,
    wd_h,
    grad_in,
    part,
    wg,
    wu,
    wd,
    x_in,
    g_in,
    x_out,
    g_out,
    gate_s,
    up_s,
    hid_s,
    dg_s,
    du_s,
    r_s,
    part_v,
    w_sem,
    x_recv,
    g_recv,
    x_send,
    g_send,
    c_send,
    o_send,
    o_recv,
    p_sem,
):
    place = lax.axis_index("section")
    side = lax.axis_index("dp_1")
    half = sections // 2
    last = sections - 1
    upper = place >= half
    width = x_in.shape[2]
    units = wg.shape[1]
    span = width // CHUNKS

    weights = [
        pltpu.make_async_copy(src, dst, w_sem.at[k])
        for k, (src, dst) in enumerate(((wg_h, wg), (wu_h, wu), (wd_h, wd)))
    ]
    for copy in weights:
        copy.start()

    @pl.when(place == 0)
    def _():
        @pl.loop(0, micro)
        def _(m):
            pltpu.make_async_copy(tok.at[m], x_in.at[m], x_recv.at[m]).start()

    next_side = jnp.where(place == half - 1, 1 - side, side)
    prev_side = jnp.where(place == half, 1 - side, side)
    after = {"section": lax.rem(place + 1, sections), "dp_1": next_side}
    before = {"section": lax.rem(place + sections - 1, sections), "dp_1": prev_side}
    partner = {"dp_1": 1 - side}

    barrier = pltpu.get_barrier_semaphore()

    @pl.when(place < last)
    def _():
        pl.semaphore_signal(barrier, inc=1, device_id=after, device_id_type=MESH)

    @pl.when(place > 0)
    def _():
        pl.semaphore_signal(barrier, inc=1, device_id=before, device_id_type=MESH)

    @pl.when(upper)
    def _():
        pl.semaphore_signal(barrier, inc=1, device_id=partner, device_id_type=MESH)

    expected = (
        jnp.where(place < last, 1, 0) + jnp.where(place > 0, 1, 0) + jnp.where(upper, 1, 0)
    )
    pl.semaphore_wait(barrier, expected)

    @pl.when(place == last)
    def _():
        @pl.loop(0, micro)
        def _(m):
            pltpu.make_async_remote_copy(
                cot.at[m], g_in.at[m], c_send, g_recv.at[m], device_id=partner, device_id_type=MESH
            ).start()

    for copy in weights:
        copy.wait()

    def forward(m):
        pltpu.make_async_copy(x_in.at[m], x_in.at[m], x_recv.at[m]).wait()
        x = x_in[m]
        gate = jnp.dot(x, wg[...], preferred_element_type=F32)
        up = jnp.dot(x, wu[...], preferred_element_type=F32)
        xf = x.astype(F32)
        r = lax.rsqrt(jnp.mean(xf * xf, axis=-1, keepdims=True) + 1e-06)
        gate = gate * r
        up = up * r
        hidden = (gate * jax.nn.sigmoid(gate) * up).astype(BF16)
        gate_s[m] = gate
        up_s[m] = up
        hid_s[m] = hidden
        r_s[m] = jnp.broadcast_to(r, (r.shape[0], 128))

        @pl.when(place < last)
        def _():
            for k in range(CHUNKS):
                cols = slice(k * span, (k + 1) * span)
                branch = lax.dot_general(
                    hidden, wd[cols, :], LAST_LAST, preferred_element_type=F32
                )
                x_out[m, :, cols] = (x_in[m, :, cols].astype(F32) + branch).astype(BF16)
                pltpu.make_async_remote_copy(
                    x_out.at[m, :, cols],
                    x_in.at[m, :, cols],
                    x_send,
                    x_recv.at[m],
                    device_id=after,
                    device_id_type=MESH,
                ).start()

    def backward(m):
        pltpu.make_async_copy(g_in.at[m], g_in.at[m], g_recv.at[m]).wait()
        d_hidden = jnp.dot(g_in[m], wd[...], preferred_element_type=F32)
        gate = gate_s[m]
        up = up_s[m]
        r = r_s[m, :, 0:1]
        sig = jax.nn.sigmoid(gate)
        d_gate = d_hidden * up * sig * (1.0 + gate * (1.0 - sig))
        d_up = d_hidden * gate * sig
        dg = d_gate.astype(BF16)
        du = d_up.astype(BF16)
        inner = jnp.sum(
            dg.astype(F32) * gate + du.astype(F32) * up, axis=-1, keepdims=True
        ) * (1.0 / width)
        shrink = r * inner
        for k in range(CHUNKS):
            cols = slice(k * span, (k + 1) * span)
            normed_grad = lax.dot_general(dg, wg[cols, :], LAST_LAST, preferred_element_type=F32)
            normed_grad = normed_grad + lax.dot_general(
                du, wu[cols, :], LAST_LAST, preferred_element_type=F32
            )
            g_out[m, :, cols] = (
                g_in[m, :, cols].astype(F32)
                + r * (normed_grad - x_in[m, :, cols].astype(F32) * shrink)
            ).astype(BF16)

            @pl.when(place > 0)
            def _():
                pltpu.make_async_remote_copy(
                    g_out.at[m, :, cols],
                    g_in.at[m, :, cols],
                    g_send,
                    g_recv.at[m],
                    device_id=before,
                    device_id_type=MESH,
                ).start()

        @pl.when(upper)
        def _():
            pltpu.make_async_remote_copy(
                g_out.at[m],
                grad_in.at[m],
                o_send,
                o_recv,
                device_id=partner,
                device_id_type=MESH,
            ).start()

        @pl.when(jnp.logical_not(upper))
        def _():
            pltpu.make_async_copy(g_out.at[m], grad_in.at[m], o_recv).start()

        dg_s[m] = (d_gate * r).astype(BF16)
        du_s[m] = (d_up * r).astype(BF16)

    lead = jnp.minimum(1 + AHEAD * (last - place), micro)

    @pl.loop(0, micro + lead)
    def _(i):
        @pl.when(i >= lead)
        def _():
            backward(i - lead)

        @pl.when(i < micro)
        def _():
            forward(i)

    rows = micro * x_in.shape[1]
    tile = 256
    dg_all = dg_s[...].reshape(rows, units)
    du_all = du_s[...].reshape(rows, units)
    hid_all = hid_s[...].reshape(rows, units)

    @pl.loop(0, width // tile)
    def _(k):
        at = pl.multiple_of(k * tile, tile)
        xs = x_in[:, :, pl.ds(at, tile)].reshape(rows, tile)
        gs = g_in[:, :, pl.ds(at, tile)].reshape(rows, tile)
        for j, (left, right) in enumerate(((xs, dg_all), (xs, du_all), (gs, hid_all))):
            part_v[pl.ds(at, tile), j * units : (j + 1) * units] = lax.dot_general(
                left, right, ROWS_ROWS, preferred_element_type=F32
            ).astype(BF16)
        pltpu.make_async_copy(
            part_v.at[pl.ds(at, tile)], part.at[pl.ds(at, tile)], p_sem
        ).start()

    pltpu.make_async_copy(part_v, part, p_sem).wait()

    @pl.when(place < last)
    def _():
        pltpu.make_async_copy(x_out, x_out, x_send).wait()

    @pl.when(place > 0)
    def _():
        pltpu.make_async_copy(g_out, g_out, g_send).wait()

    @pl.when(place == last)
    def _():
        pltpu.make_async_copy(g_in, g_in, c_send).wait()

    @pl.when(upper)
    def _():
        pltpu.make_async_copy(g_out, g_out, o_send).wait()

    pltpu.make_async_copy(g_out, grad_in, o_recv).wait()


def run_pipeline(tokens, cotangent, w_gate, w_up, w_down):
    sections = lax.axis_size("section")
    tok_rows, width = tokens.shape
    units = w_gate.shape[1]
    micro = MICRO
    rows = tok_rows // micro
    anywhere = pl.BlockSpec(memory_space=pl.ANY)
    wide = pltpu.VMEM((micro, rows, width), BF16)
    slim = pltpu.VMEM((micro, rows, units), BF16)
    slim_f = pltpu.VMEM((micro, rows, units), F32)
    weight = pltpu.VMEM((width, units), BF16)
    dma = pltpu.SemaphoreType.DMA
    grad_in, part = pl.pallas_call(
        functools.partial(pipeline_kernel, sections, micro),
        out_shape=(
            jax.ShapeDtypeStruct((micro, rows, width), BF16),
            jax.ShapeDtypeStruct((width, 3 * units), BF16),
        ),
        in_specs=[anywhere] * 5,
        out_specs=(anywhere, anywhere),
        scratch_shapes=[
            weight,
            weight,
            weight,
            wide,
            wide,
            wide,
            wide,
            slim_f,
            slim_f,
            slim,
            slim,
            slim,
            pltpu.VMEM((micro, rows, 128), F32),
            pltpu.VMEM((width, 3 * units), BF16),
            dma((3,)),
            dma((micro,)),
            dma((micro,)),
            dma,
            dma,
            dma,
            dma,
            dma,
            dma,
        ],
        compiler_params=pltpu.CompilerParams(
            collective_id=0, has_side_effects=True, vmem_limit_bytes=56 * 1024 * 1024
        ),
        name="pipeline",
    )(
        tokens.reshape(micro, rows, width),
        cotangent.reshape(micro, rows, width),
        w_gate,
        w_up,
        w_down,
    )
    return grad_in.reshape(tok_rows, width), part


def body(tokens, cotangent, w_gate, w_up, w_down):
    units = w_gate.shape[2]
    grad_in, part = run_pipeline(tokens, cotangent, w_gate[0], w_up[0], w_down[0])
    blocks = part.reshape(lax.axis_size(DP), -1, 3 * units)
    summed = reduced_to_own(blocks, DP, (2, 0, 1)).astype(F32)
    grad_g = summed[:, :units]
    grad_u = summed[:, units : 2 * units]
    grad_d = summed[:, 2 * units :]
    return (grad_in[None], grad_g[None], grad_u[None], grad_d[None])


def solution(mesh):
    torus = Mesh(
        mesh.devices.reshape(mesh.shape["section"], 8, 2, 2), ("section", "dp_0", "dp_1", "dp_2")
    )
    placed = (
        P(DP, None),
        P(DP, None),
        P("section", None, None),
        P("section", None, None),
        P("section", None, None),
    )
    return jax.shard_map(
        body,
        mesh=torus,
        in_specs=placed,
        out_specs=(
            P("section", DP, None),
            P("section", DP, None),
            P("section", DP, None),
            P("section", DP, None),
        ),
        check_vma=False,
    )
```

time: 637 us -> 258 us (0.41)
  waiting for transfers between devices: 245 us -> 90 us
  Pallas kernels: 0 us -> 143 us
  local copies, waits for them, and re-layouts: 144 us -> 8.12 us
  other arithmetic: 114 us -> 0.95 us
  starting transfers between devices: 72.8 us -> 0.12 us
  matrix products: 40 us -> 0 us
    ppermute x20 -> x0, waiting for transfers between devices: 148 us -> none  [passed_along(): return lax.ppermute(block, axis, route)]
    pallas_call x0 -> x1, Pallas kernels: none -> 143 us  [run_pipeline(): pl.pallas_call(functools.partial(pipeline_kernel, sections, micro), out_s...]
    dynamic_update_slice x60 -> x0, other arithmetic: 103 us -> none  [store_slot(): return lax.dynamic_update_index_in_dim(buffer, chosen, index, 0)]
    dynamic_slice x90 -> x0, local copies, waits for them, and re-layouts: 95 us -> none  [store_slot(): previous = lax.dynamic_index_in_dim(buffer, index, 0, keepdims=False)]
    ppermute x20 -> x0, starting transfers between devices: 72.7 us -> none  [passed_along(): return lax.ppermute(block, axis, route)]
    dot_general x21 -> x0, matrix products: 40 us -> none  [the longest x3 9.64 us: backward_layer(): jnp.dot(arriving_gradient, w_down, preferred_element_type=jnp.float32)]
    another operation x27 -> x0, local copies, waits for them, and re-layouts: 22.5 us -> none
    broadcast_in_dim x41 -> x1, local copies, waits for them, and re-layouts: 22.2 us -> 0.75 us  [body(): return (grad_in[None], grad_g[None], grad_u[None], grad_d[None])]
  transfers between devices with their start and end apart: 23 -> 3, of which waited for: 23 -> 3; matrix products, arithmetic and copies ran while one was open for 20% -> 0% of each run, Pallas kernels for 0% -> 0%
where the time goes in v1:
time: 258 us; the launch traced here: 256 us
  Pallas kernels  143 us (55%)
  waiting for transfers between devices  90 us (35%)
  between operations  13.8 us (5%)
  local copies, waits for them, and re-layouts  8.12 us (3%)
    pallas_call x1, Pallas kernels, run_pipeline(): pl.pallas_call(functools.partial(pipeline_kernel, sections, micro), out_s...  143 us
    reduce_scatter x3, waiting for transfers between devices, reduced_to_own(): blocks = lax.psum_scatter(blocks, axes[k], scatter_dimension=0, tiled=True)  89.9 us
    transpose x1, local copies, waits for them, and re-layouts, reduced_to_own(): jnp.moveaxis(blocks, sequence, range(len(axes))).reshape(-1, *inside)  6.1 us
  transfers between devices with their start and end apart: 3, of which 3 were waited for; matrix products, arithmetic and copies ran while one was open for 0% of the time, Pallas kernels for 0%

profile of v1, /device:TPU:8, one launch (start us, length us, event | category | flops | bytes accessed | tf_op | source)
XLA Modules:
  0.0 255.8 jit_solution(1638660554349112171)
XLA Ops:
  7.2 0.0 reduce-scatter.4.cloned.1.call-start
  7.2 142.9 %pipeline.1 = (bf16[15,32,2048]{2,1,0:T(8,128)(2,1)}, bf16[2048,1536]{1,0:T(8,128)(2,1)}) custom-call(bf16[15,32,2048]{2,1,0:T(8,128)(2,1)} %bitcast.24, bf16[15,32,2048]{2,1,0:T(8,128)(2,1)} %bitcast.25, bf16[2048,512]{1,0:T(8,128)(2,1)} %bitcast.21, bf16[2048,512]{1,0:T(8,128)(2,1)} %bitcast.22, bf16[2048,512]{1,0:T(8,128)(2,1)} %bitcast.23), custom_call_target="tpu_custom_call" | custom-call | tf_op jit(solution)/shard_map/pipeline/pallas_call | solution.py:274
  150.1 6.1 %copy.9 = bf16[2,8,2,64,1536]{4,3,2,1,0:T(8,128)(2,1)} copy(bf16[2,8,2,64,1536]{4,3,0,2,1:T(8,128)(2,1)} %bitcast.20) | data formatting | bytes 12582912 | tf_op jit(solution)/shard_map/transpose | solution.py:25
  156.2 0.0 reduce-scatter.4.cloned.1.call-update
  156.2 0.0 reduce-scatter.6.cloned.1.call-start
  156.3 20.2 %reduce-scatter.4.cloned.1.call-done = bf16[16,64,1536]{2,1,0:T(8,128)(2,1)} async-done(((bf16[32,64,1536]{2,1,0:T(8,128)(2,1)}), bf16[16,64,1536]{2,1,0:T(8,128)(2,1)}) %reduce-scatter.4.cloned.1.call-update) | async-done | bytes 3145744 | tf_op jit(solution)/shard_map/reduce_scatter | solution.py:27
  176.4 0.0 copy-start
  176.4 0.0 reduce-scatter.6.cloned.1.call-update
  176.4 0.0 reduce-scatter.8.cloned.1.call-start
  176.5 50.7 %reduce-scatter.6.cloned.1.call-done = bf16[2,64,1536]{2,1,0:T(8,128)(2,1)} async-done(((bf16[16,64,1536]{2,1,0:T(8,128)(2,1)}), bf16[2,64,1536]{2,1,0:T(8,128)(2,1)}) %reduce-scatter.6.cloned.1.call-update) | async-done | bytes 393232 | tf_op jit(solution)/shard_map/reduce_scatter | solution.py:27
  227.1 0.0 reduce-scatter.8.cloned.1.call-update
  227.2 19.1 %reduce-scatter.8.cloned.1.call-done = bf16[1,64,1536]{2,1,0:T(8,128)(2,1)} async-done(((bf16[2,64,1536]{2,1,0:T(8,128)(2,1)}), bf16[1,64,1536]{2,1,0:T(8,128)(2,1)}) %reduce-scatter.8.cloned.1.call-update) | async-done | bytes 196624 | tf_op jit(solution)/shard_map/reduce_scatter | solution.py:27
  246.3 1.0 bitcast_convert_fusion
  247.2 0.8 slice_bitcast_fusion
  248.0 0.0 copy-done
  248.0 1.3 copy.11
Async XLA Ops:
  7.2 169.2 %reduce-scatter.4.cloned.1.call-start = ((), (), s32[]{:S(2)}) async-start(), calls=%async_computation.3 | async-start | bytes 9437184 | tf_op jit(solution)/shard_map/reduce_scatter | solution.py:27
  156.2 70.9 %reduce-scatter.6.cloned.1.call-start = ((), (), s32[]{:S(2)}) async-start(), calls=%async_computation.4 | async-start | bytes 3538944 | tf_op jit(solution)/shard_map/reduce_scatter | solution.py:27
  176.4 71.6 %copy-start = (bf16[15,32,2048]{2,1,0:T(8,128)(2,1)S(1)}, bf16[15,32,2048]{2,1,0:T(8,128)(2,1)}, u32[]{:S(2)}) copy-start(bf16[15,32,2048]{2,1,0:T(8,128)(2,1)} %get-tuple-element.6) | copy-start | bytes 5898244
  176.4 69.8 %reduce-scatter.8.cloned.1.call-start = ((), (), s32[]{:S(2)}) async-start(), calls=%async_computation.5 | async-start | bytes 589824 | tf_op jit(solution)/shard_map/reduce_scatter | solution.py:27
Sparse Core Ops, SparseCore 0:
  156.3 20.0 reduce-scatter.3
  179.1 47.9 reduce-scatter.5
  229.8 16.4 reduce-scatter.7

commit v2 on v1

--- a/solution.py
+++ b/solution.py
@@ -11,21 +11,13 @@
 MICRO = 15
 AHEAD = 3
 CHUNKS = 2
+STREAMS = 4
 DP = ("dp_0", "dp_1", "dp_2")
 MESH = pl.DeviceIdType.MESH
 F32 = jnp.float32
 BF16 = jnp.bfloat16
 ROWS_ROWS = (((0,), (0,)), ((), ()))
 LAST_LAST = (((1,), (1,)), ((), ()))
-
-
-def reduced_to_own(blocks, axes, sequence):
-    inside = blocks.shape[1:]
-    blocks = blocks.reshape(*(lax.axis_size(a) for a in axes), *inside)
-    blocks = jnp.moveaxis(blocks, sequence, range(len(axes))).reshape(-1, *inside)
-    for k in sequence:
-        blocks = lax.psum_scatter(blocks, axes[k], scatter_dimension=0, tiled=True)
-    return blocks[0]
 
 
 def pipeline_kernel(
@@ -37,7 +29,9 @@
     wu_h,
     wd_h,
     grad_in,
-    part,
+    grad_g,
+    grad_u,
+    grad_d,
     wg,
     wu,
     wd,
@@ -51,7 +45,12 @@
     dg_s,
     du_s,
     r_s,
-    part_v,
+    part,
+    from_core,
+    ring_in,
+    ring_out,
+    side_out,
+    side_in,
     w_sem,
     x_recv,
     g_recv,
@@ -60,10 +59,18 @@
     c_send,
     o_send,
     o_recv,
-    p_sem,
+    core_send,
+    core_recv,
+    ring_send,
+    ring_recv,
+    side_send,
+    side_recv,
 ):
     place = lax.axis_index("section")
+    deep = lax.axis_index("dp_0")
     side = lax.axis_index("dp_1")
+    core = lax.axis_index("dp_2")
+    depth = part.shape[0]
     half = sections // 2
     last = sections - 1
     upper = place >= half
@@ -89,6 +96,8 @@
     after = {"section": lax.rem(place + 1, sections), "dp_1": next_side}
     before = {"section": lax.rem(place + sections - 1, sections), "dp_1": prev_side}
     partner = {"dp_1": 1 - side}
+    sibling = {"dp_2": 1 - core}
+    ring_to = ({"dp_0": lax.rem(deep + 1, depth)}, {"dp_0": lax.rem(deep + depth - 1, depth)})
 
     barrier = pltpu.get_barrier_semaphore()
 
@@ -100,13 +109,9 @@
     def _():
         pl.semaphore_signal(barrier, inc=1, device_id=before, device_id_type=MESH)
 
-    @pl.when(upper)
-    def _():
-        pl.semaphore_signal(barrier, inc=1, device_id=partner, device_id_type=MESH)
-
-    expected = (
-        jnp.where(place < last, 1, 0) + jnp.where(place > 0, 1, 0) + jnp.where(upper, 1, 0)
-    )
+    for friend in (partner, sibling, *ring_to):
+        pl.semaphore_signal(barrier, inc=1, device_id=friend, device_id_type=MESH)
+    expected = 4 + jnp.where(place < last, 1, 0) + jnp.where(place > 0, 1, 0)
     pl.semaphore_wait(barrier, expected)
 
     @pl.when(place == last)
@@ -220,25 +225,125 @@
             forward(i)
 
     rows = micro * x_in.shape[1]
-    tile = 256
+    tile = width // depth
+    own = tile // 4
     dg_all = dg_s[...].reshape(rows, units)
     du_all = du_s[...].reshape(rows, units)
     hid_all = hid_s[...].reshape(rows, units)
-
-    @pl.loop(0, width // tile)
-    def _(k):
-        at = pl.multiple_of(k * tile, tile)
+    streams = ring_in.shape[0]
+    stretch = 3 * units // streams
+
+    def weight_terms(q):
+        at = pl.multiple_of(q * tile, tile)
         xs = x_in[:, :, pl.ds(at, tile)].reshape(rows, tile)
         gs = g_in[:, :, pl.ds(at, tile)].reshape(rows, tile)
         for j, (left, right) in enumerate(((xs, dg_all), (xs, du_all), (gs, hid_all))):
-            part_v[pl.ds(at, tile), j * units : (j + 1) * units] = lax.dot_general(
-                left, right, ROWS_ROWS, preferred_element_type=F32
-            ).astype(BF16)
-        pltpu.make_async_copy(
-            part_v.at[pl.ds(at, tile)], part.at[pl.ds(at, tile)], p_sem
+            term = lax.dot_general(left, right, ROWS_ROWS, preferred_element_type=F32)
+            part[q, :, :, :, j * units : (j + 1) * units] = term.astype(BF16).reshape(
+                2, 2, own, units
+            )
+        for k in range(2):
+            pltpu.make_async_remote_copy(
+                part.at[q, k, 1 - core],
+                from_core.at[q, k],
+                core_send,
+                core_recv.at[q],
+                device_id=sibling,
+                device_id_type=MESH,
+            ).start()
+
+    def chip_sum(q, cols):
+        return part[q, :, core, :, cols].astype(F32) + from_core[q, :, :, cols].astype(F32)
+
+    def both_ways(step):
+        return (
+            lax.rem(deep + 2 * depth - 1 - step, depth),
+            lax.rem(deep + 1 + step, depth),
+        )
+
+    for q in both_ways(0):
+        weight_terms(q)
+
+    @pl.loop(0, depth - 1)
+    def _(step):
+        down, up = both_ways(step)
+
+        @pl.when(step < depth // 2 - 1)
+        def _():
+            first, second = both_ways(step + 1)
+            weight_terms(first)
+            weight_terms(jnp.where(step == depth // 2 - 2, deep, second))
+
+        @pl.when(step < depth // 2)
+        def _():
+            pltpu.make_async_copy(from_core.at[down], from_core.at[down], core_recv.at[down]).wait()
+
+        @pl.when(step < depth // 2 - 1)
+        def _():
+            pltpu.make_async_copy(from_core.at[up], from_core.at[up], core_recv.at[up]).wait()
+
+        for n in range(streams):
+            q = (down, up)[n % 2]
+            cols = slice(n * stretch, (n + 1) * stretch)
+            total = chip_sum(q, cols)
+
+            @pl.when(step == 0)
+            def _():
+                ring_out[n, step] = total.astype(BF16)
+
+            @pl.when(step > 0)
+            def _():
+                pltpu.make_async_copy(
+                    ring_in.at[n, step - 1], ring_in.at[n, step - 1], ring_recv.at[n, step - 1]
+                ).wait()
+                ring_out[n, step] = (total + ring_in[n, step - 1].astype(F32)).astype(BF16)
+
+            pltpu.make_async_remote_copy(
+                ring_out.at[n, step],
+                ring_in.at[n, step],
+                ring_send.at[n],
+                ring_recv.at[n, step],
+                device_id=ring_to[n % 2],
+                device_id_type=MESH,
+            ).start()
+
+    pltpu.make_async_copy(from_core.at[deep], from_core.at[deep], core_recv.at[deep]).wait()
+    end = depth - 2
+    for n in range(streams):
+        cols = slice(n * stretch, (n + 1) * stretch)
+        pltpu.make_async_copy(ring_in.at[n, end], ring_in.at[n, end], ring_recv.at[n, end]).wait()
+        side_out[n] = (
+            part[deep, 1 - side, core, :, cols].astype(F32)
+            + from_core[deep, 1 - side, :, cols].astype(F32)
+            + ring_in[n, end, 1 - side].astype(F32)
+        ).astype(BF16)
+        pltpu.make_async_remote_copy(
+            side_out.at[n],
+            side_in.at[n],
+            side_send,
+            side_recv.at[n],
+            device_id=partner,
+            device_id_type=MESH,
         ).start()
-
-    pltpu.make_async_copy(part_v, part, p_sem).wait()
+    whole = []
+    for n in range(streams):
+        cols = slice(n * stretch, (n + 1) * stretch)
+        pltpu.make_async_copy(side_in.at[n], side_in.at[n], side_recv.at[n]).wait()
+        whole.append(
+            part[deep, side, core, :, cols].astype(F32)
+            + from_core[deep, side, :, cols].astype(F32)
+            + ring_in[n, end, side].astype(F32)
+            + side_in[n].astype(F32)
+        )
+    whole = jnp.concatenate(whole, axis=1)
+    grad_g[...] = whole[:, :units]
+    grad_u[...] = whole[:, units : 2 * units]
+    grad_d[...] = whole[:, 2 * units :]
+
+    pltpu.make_async_copy(side_out, side_out, side_send).wait()
+    pltpu.make_async_copy(from_core, from_core, core_send).wait()
+    for n in range(streams):
+        pltpu.make_async_copy(ring_out.at[n], ring_out.at[n], ring_send.at[n]).wait()
 
     @pl.when(place < last)
     def _():
@@ -271,14 +376,20 @@
     slim_f = pltpu.VMEM((micro, rows, units), F32)
     weight = pltpu.VMEM((width, units), BF16)
     dma = pltpu.SemaphoreType.DMA
-    grad_in, part = pl.pallas_call(
+    grad = jax.ShapeDtypeStruct((width // lax.axis_size(DP), units), F32)
+    streams, depth = STREAMS, lax.axis_size("dp_0")
+    own, stretch = width // (4 * depth), 3 * units // streams
+    vmem = pl.BlockSpec(memory_space=pltpu.VMEM)
+    grad_in, *grads = pl.pallas_call(
         functools.partial(pipeline_kernel, sections, micro),
         out_shape=(
             jax.ShapeDtypeStruct((micro, rows, width), BF16),
-            jax.ShapeDtypeStruct((width, 3 * units), BF16),
+            grad,
+            grad,
+            grad,
         ),
         in_specs=[anywhere] * 5,
-        out_specs=(anywhere, anywhere),
+        out_specs=(anywhere, vmem, vmem, vmem),
         scratch_shapes=[
             weight,
             weight,
@@ -293,7 +404,12 @@
             slim,
             slim,
             pltpu.VMEM((micro, rows, 128), F32),
-            pltpu.VMEM((width, 3 * units), BF16),
+            pltpu.VMEM((depth, 2, 2, own, 3 * units), BF16),
+            pltpu.VMEM((depth, 2, own, 3 * units), BF16),
+            pltpu.VMEM((streams, depth - 1, 2, own, stretch), BF16),
+            pltpu.VMEM((streams, depth - 1, 2, own, stretch), BF16),
+            pltpu.VMEM((streams, own, stretch), BF16),
+            pltpu.VMEM((streams, own, stretch), BF16),
             dma((3,)),
             dma((micro,)),
             dma((micro,)),
@@ -303,6 +419,11 @@
             dma,
             dma,
             dma,
+            dma((depth,)),
+            dma((streams,)),
+            dma((streams, depth - 1)),
+            dma,
+            dma((streams,)),
         ],
         compiler_params=pltpu.CompilerParams(
             collective_id=0, has_side_effects=True, vmem_limit_bytes=56 * 1024 * 1024
@@ -315,18 +436,12 @@
         w_up,
         w_down,
     )
-    return grad_in.reshape(tok_rows, width), part
+    return grad_in.reshape(tok_rows, width), *grads
 
 
 def body(tokens, cotangent, w_gate, w_up, w_down):
-    units = w_gate.shape[2]
-    grad_in, part = run_pipeline(tokens, cotangent, w_gate[0], w_up[0], w_down[0])
-    blocks = part.reshape(lax.axis_size(DP), -1, 3 * units)
-    summed = reduced_to_own(blocks, DP, (2, 0, 1)).astype(F32)
-    grad_g = summed[:, :units]
-    grad_u = summed[:, units : 2 * units]
-    grad_d = summed[:, 2 * units :]
-    return (grad_in[None], grad_g[None], grad_u[None], grad_d[None])
+    outs = run_pipeline(tokens, cotangent, w_gate[0], w_up[0], w_down[0])
+    return tuple(out[None] for out in outs)
 
 
 def solution(mesh):

time: 258 us -> 190 us (0.74)
  waiting for transfers between devices: 90 us -> 0 us
  Pallas kernels: 143 us -> 184 us
  between operations: 13.8 us -> 0.67 us
  local copies, waits for them, and re-layouts: 8.12 us -> 5.07 us
    reduce_scatter x3 -> x0, waiting for transfers between devices: 89.9 us -> none  [reduced_to_own(): blocks = lax.psum_scatter(blocks, axes[k], scatter_dimension=0, tiled=True)]
    pallas_call x1, Pallas kernels: 143 us -> 184 us  [run_pipeline(): pl.pallas_call(functools.partial(pipeline_kernel, sections, micro), out_s...]
    transpose x1 -> x0, local copies, waits for them, and re-layouts: 6.1 us -> none  [reduced_to_own(): jnp.moveaxis(blocks, sequence, range(len(axes))).reshape(-1, *inside)]
    unnamed x3 -> x10, local copies, waits for them, and re-layouts: 1.28 us -> 5.07 us
  transfers between devices with their start and end apart: 3 -> 0, of which waited for: 3 -> 0; matrix products, arithmetic and copies ran while one was open for 0% -> 0% of each run, Pallas kernels for 0% -> 0%
where the time goes in v2:
time: 190 us
  Pallas kernels  184 us (97%)
  local copies, waits for them, and re-layouts  5.07 us (3%)
    pallas_call x1, Pallas kernels, run_pipeline(): pl.pallas_call(functools.partial(pipeline_kernel, sections, micro), out_s...  184 us
    unnamed x10, local copies, waits for them, and re-layouts  5.07 us

profile of v2, /device:TPU:8, one launch (start us, length us, event | category | flops | bytes accessed | tf_op | source)
XLA Modules:
  0.0 190.0 jit_solution(14482888295735921012)
XLA Ops:
  0.6 184.3 %pipeline.1 = (bf16[15,32,2048]{2,1,0:T(8,128)(2,1)}, f32[64,512]{1,0:T(8,128)}, f32[64,512]{1,0:T(8,128)}, f32[64,512]{1,0:T(8,128)}) custom-call(bf16[15,32,2048]{2,1,0:T(8,128)(2,1)} %bitcast.12, bf16[15,32,2048]{2,1,0:T(8,128)(2,1)} %bitcast.13, bf16[2048,512]{1,0:T(8,128)(2,1)} %bitcast.9, bf16[2048,512]{1,0:T(8,128)(2,1)} %bitcast.10, ...), custom_call_target="tpu_custom_call" | custom-call | tf_op jit(solution)/shard_map/pipeline/pallas_call | solution.py:383
  184.9 0.0 copy-start.2
  184.9 0.0 copy-start.1
  184.9 0.0 copy-start
  184.9 3.1 %copy.13 = bf16[1,480,2048]{2,1,0:T(8,128)(2,1)} copy(bf16[1,480,2048]{2,1,0:T(8,128)(2,1)} %bitcast.14) | data formatting | bytes 3932160
  188.0 0.0 copy-done.2
  188.0 0.7 copy.14
  188.7 0.0 copy-done.1
  188.7 0.7 copy.15
  189.3 0.0 copy-done
  189.3 0.7 copy.16
Async XLA Ops:
  184.9 3.1 %copy-start.2 = (f32[64,512]{1,0:T(8,128)S(1)}, f32[64,512]{1,0:T(8,128)}, u32[]{:S(2)}) copy-start(f32[64,512]{1,0:T(8,128)} %get-tuple-element.9) | copy-start | bytes 393220
  184.9 3.8 %copy-start.1 = (f32[64,512]{1,0:T(8,128)S(1)}, f32[64,512]{1,0:T(8,128)}, u32[]{:S(2)}) copy-start(f32[64,512]{1,0:T(8,128)} %get-tuple-element.10) | copy-start | bytes 393220
  184.9 4.4 %copy-start = (f32[64,512]{1,0:T(8,128)S(1)}, f32[64,512]{1,0:T(8,128)}, u32[]{:S(2)}) copy-start(f32[64,512]{1,0:T(8,128)} %get-tuple-element.11) | copy-start | bytes 393220

commit v3 on v2

--- a/solution.py
+++ b/solution.py
@@ -9,7 +9,7 @@
 from jax.sharding import PartitionSpec as P
 
 MICRO = 15
-AHEAD = 3
+AHEAD = 4
 CHUNKS = 2
 STREAMS = 4
 DP = ("dp_0", "dp_1", "dp_2")
@@ -17,7 +17,6 @@
 F32 = jnp.float32
 BF16 = jnp.bfloat16
 ROWS_ROWS = (((0,), (0,)), ((), ()))
-LAST_LAST = (((1,), (1,)), ((), ()))
 
 
 def pipeline_kernel(
@@ -35,6 +34,8 @@
     wg,
     wu,
     wd,
+    wd_t,
+    wgu_t,
     x_in,
     g_in,
     x_out,
@@ -42,8 +43,7 @@
     gate_s,
     up_s,
     hid_s,
-    dg_s,
-    du_s,
+    dgu_s,
     r_s,
     part,
     from_core,
@@ -52,6 +52,7 @@
     side_out,
     side_in,
     w_sem,
+    turn,
     x_recv,
     g_recv,
     x_send,
@@ -80,7 +81,7 @@
 
     weights = [
         pltpu.make_async_copy(src, dst, w_sem.at[k])
-        for k, (src, dst) in enumerate(((wg_h, wg), (wu_h, wu), (wd_h, wd)))
+        for k, (src, dst) in enumerate(((wd_h, wd), (wg_h, wg), (wu_h, wu)))
     ]
     for copy in weights:
         copy.start()
@@ -122,8 +123,26 @@
                 cot.at[m], g_in.at[m], c_send, g_recv.at[m], device_id=partner, device_id_type=MESH
             ).start()
 
-    for copy in weights:
-        copy.wait()
+    block = width // depth
+
+    def turned(src, dst, base):
+        @pl.loop(0, depth)
+        def _(k):
+            at = pl.multiple_of(k * block, block)
+            dst[base : base + units, pl.ds(at, block)] = src[pl.ds(at, block), :].T
+
+    def turn_gate_up():
+        turned(wg, wgu_t, 0)
+        turned(wu, wgu_t, units)
+
+    weights[0].wait()
+    turned(wd, wd_t, 0)
+    weights[1].wait()
+    weights[2].wait()
+
+    @pl.when(place > 0)
+    def _():
+        turn_gate_up()
 
     def forward(m):
         pltpu.make_async_copy(x_in.at[m], x_in.at[m], x_recv.at[m]).wait()
@@ -144,9 +163,7 @@
         def _():
             for k in range(CHUNKS):
                 cols = slice(k * span, (k + 1) * span)
-                branch = lax.dot_general(
-                    hidden, wd[cols, :], LAST_LAST, preferred_element_type=F32
-                )
+                branch = jnp.dot(hidden, wd_t[:, cols], preferred_element_type=F32)
                 x_out[m, :, cols] = (x_in[m, :, cols].astype(F32) + branch).astype(BF16)
                 pltpu.make_async_remote_copy(
                     x_out.at[m, :, cols],
@@ -172,12 +189,10 @@
             dg.astype(F32) * gate + du.astype(F32) * up, axis=-1, keepdims=True
         ) * (1.0 / width)
         shrink = r * inner
+        dgu = jnp.concatenate([dg, du], axis=1)
         for k in range(CHUNKS):
             cols = slice(k * span, (k + 1) * span)
-            normed_grad = lax.dot_general(dg, wg[cols, :], LAST_LAST, preferred_element_type=F32)
-            normed_grad = normed_grad + lax.dot_general(
-                du, wu[cols, :], LAST_LAST, preferred_element_type=F32
-            )
+            normed_grad = jnp.dot(dgu, wgu_t[:, cols], preferred_element_type=F32)
             g_out[m, :, cols] = (
                 g_in[m, :, cols].astype(F32)
                 + r * (normed_grad - x_in[m, :, cols].astype(F32) * shrink)
@@ -209,26 +224,37 @@
         def _():
             pltpu.make_async_copy(g_out.at[m], grad_in.at[m], o_recv).start()
 
-        dg_s[m] = (d_gate * r).astype(BF16)
-        du_s[m] = (d_up * r).astype(BF16)
+        dgu_s[m, :, :units] = (d_gate * r).astype(BF16)
+        dgu_s[m, :, units:] = (d_up * r).astype(BF16)
 
     lead = jnp.minimum(1 + AHEAD * (last - place), micro)
 
     @pl.loop(0, micro + lead)
     def _(i):
+        @pl.when((i == lead) & (place == 0))
+        def _():
+            turn_gate_up()
+
         @pl.when(i >= lead)
         def _():
             backward(i - lead)
 
+        @pl.when((i == 0) & (place == 0) & (core == 1))
+        def _():
+            pl.semaphore_wait(turn, 1)
+
         @pl.when(i < micro)
         def _():
             forward(i)
+
+        @pl.when((i == 0) & (place == 0) & (core == 0))
+        def _():
+            pl.semaphore_signal(turn, inc=1, device_id=sibling, device_id_type=MESH)
 
     rows = micro * x_in.shape[1]
     tile = width // depth
     own = tile // 4
-    dg_all = dg_s[...].reshape(rows, units)
-    du_all = du_s[...].reshape(rows, units)
+    dgu_all = dgu_s[...].reshape(rows, 2 * units)
     hid_all = hid_s[...].reshape(rows, units)
     streams = ring_in.shape[0]
     stretch = 3 * units // streams
@@ -237,11 +263,10 @@
         at = pl.multiple_of(q * tile, tile)
         xs = x_in[:, :, pl.ds(at, tile)].reshape(rows, tile)
         gs = g_in[:, :, pl.ds(at, tile)].reshape(rows, tile)
-        for j, (left, right) in enumerate(((xs, dg_all), (xs, du_all), (gs, hid_all))):
+        for left, right, low in ((xs, dgu_all, 0), (gs, hid_all, 2 * units)):
             term = lax.dot_general(left, right, ROWS_ROWS, preferred_element_type=F32)
-            part[q, :, :, :, j * units : (j + 1) * units] = term.astype(BF16).reshape(
-                2, 2, own, units
-            )
+            high = low + right.shape[1]
+            part[q, :, :, :, low:high] = term.astype(BF16).reshape(2, 2, own, high - low)
         for k in range(2):
             pltpu.make_async_remote_copy(
                 part.at[q, k, 1 - core],
@@ -394,6 +419,8 @@
             weight,
             weight,
             weight,
+            pltpu.VMEM((units, width), BF16),
+            pltpu.VMEM((2 * units, width), BF16),
             wide,
             wide,
             wide,
@@ -401,8 +428,7 @@
             slim_f,
             slim_f,
             slim,
-            slim,
-            slim,
+            pltpu.VMEM((micro, rows, 2 * units), BF16),
             pltpu.VMEM((micro, rows, 128), F32),
             pltpu.VMEM((depth, 2, 2, own, 3 * units), BF16),
             pltpu.VMEM((depth, 2, own, 3 * units), BF16),
@@ -411,6 +437,7 @@
             pltpu.VMEM((streams, own, stretch), BF16),
             pltpu.VMEM((streams, own, stretch), BF16),
             dma((3,)),
+            pltpu.SemaphoreType.REGULAR,
             dma((micro,)),
             dma((micro,)),
             dma,

time: 190 us -> 179 us (0.942)
  Pallas kernels: 184 us -> 173 us
    pallas_call x1, Pallas kernels: 184 us -> 173 us  [run_pipeline(): pl.pallas_call(functools.partial(pipeline_kernel, sections, micro), out_s...]
where the time goes in v3:
time: 179 us
  Pallas kernels  173 us (97%)
  local copies, waits for them, and re-layouts  5.07 us (3%)
    pallas_call x1, Pallas kernels, run_pipeline(): pl.pallas_call(functools.partial(pipeline_kernel, sections, micro), out_s...  173 us
    unnamed x10, local copies, waits for them, and re-layouts  5.07 us

profile of v3, /device:TPU:8, one launch (start us, length us, event | category | flops | bytes accessed | tf_op | source)
XLA Modules:
  0.0 179.0 jit_solution(16843943074960065406)
XLA Ops:
  0.6 173.2 %pipeline.1 = (bf16[15,32,2048]{2,1,0:T(8,128)(2,1)}, f32[64,512]{1,0:T(8,128)}, f32[64,512]{1,0:T(8,128)}, f32[64,512]{1,0:T(8,128)}) custom-call(bf16[15,32,2048]{2,1,0:T(8,128)(2,1)} %bitcast.12, bf16[15,32,2048]{2,1,0:T(8,128)(2,1)} %bitcast.13, bf16[2048,512]{1,0:T(8,128)(2,1)} %bitcast.9, bf16[2048,512]{1,0:T(8,128)(2,1)} %bitcast.10, ...), custom_call_target="tpu_custom_call" | custom-call | tf_op jit(solution)/shard_map/pipeline/pallas_call | solution.py:408
  173.9 0.0 copy-start.2
  173.9 0.0 copy-start.1
  173.9 0.0 copy-start
  173.9 3.1 %copy.13 = bf16[1,480,2048]{2,1,0:T(8,128)(2,1)} copy(bf16[1,480,2048]{2,1,0:T(8,128)(2,1)} %bitcast.14) | data formatting | bytes 3932160
  177.0 0.0 copy-done.2
  177.0 0.7 copy.14
  177.6 0.0 copy-done.1
  177.6 0.7 copy.15
  178.3 0.0 copy-done
  178.3 0.7 copy.16
Async XLA Ops:
  173.9 3.1 %copy-start.2 = (f32[64,512]{1,0:T(8,128)S(1)}, f32[64,512]{1,0:T(8,128)}, u32[]{:S(2)}) copy-start(f32[64,512]{1,0:T(8,128)} %get-tuple-element.9) | copy-start | bytes 393220
  173.9 3.8 %copy-start.1 = (f32[64,512]{1,0:T(8,128)S(1)}, f32[64,512]{1,0:T(8,128)}, u32[]{:S(2)}) copy-start(f32[64,512]{1,0:T(8,128)} %get-tuple-element.10) | copy-start | bytes 393220
  173.9 4.4 %copy-start = (f32[64,512]{1,0:T(8,128)S(1)}, f32[64,512]{1,0:T(8,128)}, u32[]{:S(2)}) copy-start(f32[64,512]{1,0:T(8,128)} %get-tuple-element.11) | copy-start | bytes 393220

commit v4 on v3

--- a/solution.py
+++ b/solution.py
@@ -12,6 +12,8 @@
 AHEAD = 4
 CHUNKS = 2
 STREAMS = 4
+SIDE_FIRST = 2
+PIECES = 5
 DP = ("dp_0", "dp_1", "dp_2")
 MESH = pl.DeviceIdType.MESH
 F32 = jnp.float32
@@ -51,6 +53,8 @@
     ring_out,
     side_out,
     side_in,
+    end_out,
+    end_in,
     w_sem,
     turn,
     x_recv,
@@ -66,6 +70,8 @@
     ring_recv,
     side_send,
     side_recv,
+    end_send,
+    end_recv,
 ):
     place = lax.axis_index("section")
     deep = lax.axis_index("dp_0")
@@ -78,6 +84,7 @@
     width = x_in.shape[2]
     units = wg.shape[1]
     span = width // CHUNKS
+    chunks = [slice(k * span, (k + 1) * span) for k in range(CHUNKS)]
 
     weights = [
         pltpu.make_async_copy(src, dst, w_sem.at[k])
@@ -161,8 +168,7 @@
 
         @pl.when(place < last)
         def _():
-            for k in range(CHUNKS):
-                cols = slice(k * span, (k + 1) * span)
+            for k, cols in enumerate(chunks):
                 branch = jnp.dot(hidden, wd_t[:, cols], preferred_element_type=F32)
                 x_out[m, :, cols] = (x_in[m, :, cols].astype(F32) + branch).astype(BF16)
                 pltpu.make_async_remote_copy(
@@ -190,8 +196,7 @@
         ) * (1.0 / width)
         shrink = r * inner
         dgu = jnp.concatenate([dg, du], axis=1)
-        for k in range(CHUNKS):
-            cols = slice(k * span, (k + 1) * span)
+        for k, cols in enumerate(chunks):
             normed_grad = jnp.dot(dgu, wgu_t[:, cols], preferred_element_type=F32)
             g_out[m, :, cols] = (
                 g_in[m, :, cols].astype(F32)
@@ -256,10 +261,16 @@
     own = tile // 4
     dgu_all = dgu_s[...].reshape(rows, 2 * units)
     hid_all = hid_s[...].reshape(rows, units)
-    streams = ring_in.shape[0]
-    stretch = 3 * units // streams
-
-    def weight_terms(q):
+    streams, stretch = ring_in.shape[0], ring_in.shape[-1]
+    first_b = SIDE_FIRST
+    middle = depth // 2
+
+    def tile_at(j):
+        turn_off = jnp.where(lax.rem(j, 2) == 1, middle - (j + 1) // 2, j // 2 + middle)
+        return lax.rem(deep + jnp.where(j == depth - 1, 0, turn_off), depth)
+
+    def weight_terms(j):
+        q = tile_at(j)
         at = pl.multiple_of(q * tile, tile)
         xs = x_in[:, :, pl.ds(at, tile)].reshape(rows, tile)
         gs = g_in[:, :, pl.ds(at, tile)].reshape(rows, tile)
@@ -277,98 +288,145 @@
                 device_id_type=MESH,
             ).start()
 
-    def chip_sum(q, cols):
-        return part[q, :, core, :, cols].astype(F32) + from_core[q, :, :, cols].astype(F32)
-
-    def both_ways(step):
-        return (
-            lax.rem(deep + 2 * depth - 1 - step, depth),
-            lax.rem(deep + 1 + step, depth),
-        )
-
-    for q in both_ways(0):
-        weight_terms(q)
-
-    @pl.loop(0, depth - 1)
-    def _(step):
-        down, up = both_ways(step)
-
-        @pl.when(step < depth // 2 - 1)
-        def _():
-            first, second = both_ways(step + 1)
-            weight_terms(first)
-            weight_terms(jnp.where(step == depth // 2 - 2, deep, second))
-
-        @pl.when(step < depth // 2)
-        def _():
-            pltpu.make_async_copy(from_core.at[down], from_core.at[down], core_recv.at[down]).wait()
-
-        @pl.when(step < depth // 2 - 1)
-        def _():
-            pltpu.make_async_copy(from_core.at[up], from_core.at[up], core_recv.at[up]).wait()
-
-        for n in range(streams):
-            q = (down, up)[n % 2]
-            cols = slice(n * stretch, (n + 1) * stretch)
-            total = chip_sum(q, cols)
-
-            @pl.when(step == 0)
-            def _():
-                ring_out[n, step] = total.astype(BF16)
-
-            @pl.when(step > 0)
-            def _():
-                pltpu.make_async_copy(
-                    ring_in.at[n, step - 1], ring_in.at[n, step - 1], ring_recv.at[n, step - 1]
-                ).wait()
-                ring_out[n, step] = (total + ring_in[n, step - 1].astype(F32)).astype(BF16)
-
-            pltpu.make_async_remote_copy(
-                ring_out.at[n, step],
-                ring_in.at[n, step],
-                ring_send.at[n],
-                ring_recv.at[n, step],
-                device_id=ring_to[n % 2],
-                device_id_type=MESH,
-            ).start()
-
-    pltpu.make_async_copy(from_core.at[deep], from_core.at[deep], core_recv.at[deep]).wait()
-    end = depth - 2
-    for n in range(streams):
-        cols = slice(n * stretch, (n + 1) * stretch)
-        pltpu.make_async_copy(ring_in.at[n, end], ring_in.at[n, end], ring_recv.at[n, end]).wait()
-        side_out[n] = (
-            part[deep, 1 - side, core, :, cols].astype(F32)
-            + from_core[deep, 1 - side, :, cols].astype(F32)
-            + ring_in[n, end, 1 - side].astype(F32)
-        ).astype(BF16)
+    def terms(low, high):
+        @pl.loop(low, high)
+        def _(j):
+            weight_terms(j)
+
+    def columns(n):
+        return slice(n * stretch, (n + 1) * stretch)
+
+    def chip_sum(q, k, cols):
+        return part[q, k, core, :, cols].astype(F32) + from_core[q, k, :, cols].astype(F32)
+
+    side_cols = slice(0, first_b * stretch)
+
+    def chip_ready(j):
+        q = tile_at(j)
+        pltpu.make_async_copy(from_core.at[q], from_core.at[q], core_recv.at[q]).wait()
+        side_out[q] = chip_sum(q, 1 - side, side_cols).astype(BF16)
         pltpu.make_async_remote_copy(
-            side_out.at[n],
-            side_in.at[n],
+            side_out.at[q],
+            side_in.at[q],
             side_send,
-            side_recv.at[n],
+            side_recv.at[q],
             device_id=partner,
             device_id_type=MESH,
         ).start()
-    whole = []
-    for n in range(streams):
-        cols = slice(n * stretch, (n + 1) * stretch)
-        pltpu.make_async_copy(side_in.at[n], side_in.at[n], side_recv.at[n]).wait()
-        whole.append(
-            part[deep, side, core, :, cols].astype(F32)
-            + from_core[deep, side, :, cols].astype(F32)
-            + ring_in[n, end, side].astype(F32)
-            + side_in[n].astype(F32)
+
+    def side_ready(j):
+        q = tile_at(j)
+        pltpu.make_async_copy(side_in.at[q], side_in.at[q], side_recv.at[q]).wait()
+
+    def own_sums(n, q):
+        if n < first_b:
+            return [(0, chip_sum(q, side, columns(n)) + side_in[q, :, columns(n)].astype(F32))]
+        return [(k, chip_sum(q, k, columns(n))) for k in range(2)]
+
+    def slot(ref, n, way, step):
+        return ref.at[n, way, step, 0] if n < first_b else ref.at[n, way, step]
+
+    def ring_wait(n, way, step):
+        ref = slot(ring_in, n, way, step)
+        pltpu.make_async_copy(ref, ref, ring_recv.at[n, way, step]).wait()
+
+    def ring_step(step, group):
+        for long in (True, False):
+            for n in group:
+                for way in range(2):
+                    if (n % 2 == way) != long or (step == 0 and not long):
+                        continue
+                    q = lax.rem(deep + (middle - step if way == 0 else middle + step), depth)
+                    held = step > (0 if long else 1)
+                    if held:
+                        ring_wait(n, way, step - 1)
+                    for k, total in own_sums(n, q):
+                        if held:
+                            total = total + ring_in[n, way, step - 1, k].astype(F32)
+                        ring_out[n, way, step, k] = total.astype(BF16)
+                    pltpu.make_async_remote_copy(
+                        slot(ring_out, n, way, step),
+                        slot(ring_in, n, way, step),
+                        ring_send.at[n, way],
+                        ring_recv.at[n, way, step],
+                        device_id=ring_to[way],
+                        device_id_type=MESH,
+                    ).start()
+
+    def arrived(n, k):
+        return ring_in[n, 0, middle - 1, k].astype(F32) + ring_in[n, 1, middle - 1, k].astype(F32)
+
+    group_a, group_b = range(first_b), range(first_b, streams)
+    terms(0, 2)
+    chip_ready(0)
+    ring_step(0, group_b)
+    terms(2, 4)
+    chip_ready(1)
+    chip_ready(2)
+    ring_step(1, group_b)
+    terms(4, 6)
+    chip_ready(3)
+    chip_ready(4)
+    side_ready(0)
+    ring_step(0, group_a)
+    ring_step(2, group_b)
+    terms(6, 8)
+    chip_ready(5)
+    chip_ready(6)
+    side_ready(1)
+    side_ready(2)
+    ring_step(1, group_a)
+    ring_step(3, group_b)
+    chip_ready(7)
+    side_ready(3)
+    side_ready(4)
+    ring_step(2, group_a)
+    for n in group_b:
+        for way in range(2):
+            ring_wait(n, way, middle - 1)
+        end_out[n - first_b] = (
+            chip_sum(deep, 1 - side, columns(n)) + arrived(n, 1 - side)
+        ).astype(BF16)
+        pltpu.make_async_remote_copy(
+            end_out.at[n - first_b],
+            end_in.at[n - first_b],
+            end_send,
+            end_recv.at[n - first_b],
+            device_id=partner,
+            device_id_type=MESH,
+        ).start()
+    side_ready(5)
+    side_ready(6)
+    ring_step(3, group_a)
+    side_ready(7)
+    whole = {}
+    for n in group_b:
+        ref = end_in.at[n - first_b]
+        pltpu.make_async_copy(ref, ref, end_recv.at[n - first_b]).wait()
+        whole[n] = (
+            chip_sum(deep, side, columns(n))
+            + arrived(n, side)
+            + end_in[n - first_b].astype(F32)
         )
-    whole = jnp.concatenate(whole, axis=1)
+    for n in group_a:
+        for way in range(2):
+            ring_wait(n, way, middle - 1)
+        whole[n] = own_sums(n, deep)[0][1] + arrived(n, 0)
+    whole = jnp.concatenate([whole[n] for n in range(streams)], axis=1)
     grad_g[...] = whole[:, :units]
     grad_u[...] = whole[:, units : 2 * units]
     grad_d[...] = whole[:, 2 * units :]
 
     pltpu.make_async_copy(side_out, side_out, side_send).wait()
+    pltpu.make_async_copy(end_out, end_out, end_send).wait()
     pltpu.make_async_copy(from_core, from_core, core_send).wait()
     for n in range(streams):
-        pltpu.make_async_copy(ring_out.at[n], ring_out.at[n], ring_send.at[n]).wait()
+        for way in range(2):
+            lowest = 0 if n % 2 == way else 1
+            sent = ring_out.at[n, way, lowest:middle]
+            if n < first_b:
+                sent = ring_out.at[n, way, lowest:middle, 0]
+            pltpu.make_async_copy(sent, sent, ring_send.at[n, way]).wait()
 
     @pl.when(place < last)
     def _():
@@ -387,6 +445,43 @@
         pltpu.make_async_copy(g_out, g_out, o_send).wait()
 
     pltpu.make_async_copy(g_out, grad_in, o_recv).wait()
+
+
+def finish_kernel(wide_in, g_in, u_in, d_in, wide_out, g_out, u_out, d_out, wide, slim, into, out):
+    size = wide.shape[0] // PIECES
+    routes = [
+        (wide_in.at[pl.ds(k * size, size)], wide.at[pl.ds(k * size, size)],
+         wide_out.at[pl.ds(k * size, size)])
+        for k in range(PIECES)
+    ]
+    for k, (src, dst) in enumerate(((g_in, g_out), (u_in, u_out), (d_in, d_out))):
+        routes.append((src, slim.at[k], dst))
+    for k, (src, held, _) in enumerate(routes):
+        pltpu.make_async_copy(src, held, into.at[k]).start()
+    for k, (src, held, dst) in enumerate(routes):
+        pltpu.make_async_copy(src, held, into.at[k]).wait()
+        pltpu.make_async_copy(held, dst, out.at[k]).start()
+    for k, (_, held, dst) in enumerate(routes):
+        pltpu.make_async_copy(held, dst, out.at[k]).wait()
+
+
+def finished(wide, *slim):
+    anywhere = pl.BlockSpec(memory_space=pl.ANY)
+    arrays = (wide, *slim)
+    return pl.pallas_call(
+        finish_kernel,
+        out_shape=tuple(jax.ShapeDtypeStruct(a.shape, a.dtype) for a in arrays),
+        in_specs=[anywhere] * 4,
+        out_specs=(anywhere,) * 4,
+        scratch_shapes=[
+            pltpu.VMEM(wide.shape, wide.dtype),
+            pltpu.VMEM((3, *slim[0].shape), F32),
+            pltpu.SemaphoreType.DMA((PIECES + 3,)),
+            pltpu.SemaphoreType.DMA((PIECES + 3,)),
+        ],
+        compiler_params=pltpu.CompilerParams(vmem_limit_bytes=60 * 1024 * 1024),
+        name="finish",
+    )(*arrays)
 
 
 def run_pipeline(tokens, cotangent, w_gate, w_up, w_down):
@@ -432,10 +527,12 @@
             pltpu.VMEM((micro, rows, 128), F32),
             pltpu.VMEM((depth, 2, 2, own, 3 * units), BF16),
             pltpu.VMEM((depth, 2, own, 3 * units), BF16),
-            pltpu.VMEM((streams, depth - 1, 2, own, stretch), BF16),
-            pltpu.VMEM((streams, depth - 1, 2, own, stretch), BF16),
-            pltpu.VMEM((streams, own, stretch), BF16),
-            pltpu.VMEM((streams, own, stretch), BF16),
+            pltpu.VMEM((streams, 2, depth // 2, 2, own, stretch), BF16),
+            pltpu.VMEM((streams, 2, depth // 2, 2, own, stretch), BF16),
+            pltpu.VMEM((depth, own, SIDE_FIRST * stretch), BF16),
+            pltpu.VMEM((depth, own, SIDE_FIRST * stretch), BF16),
+            pltpu.VMEM((streams - SIDE_FIRST, own, stretch), BF16),
+            pltpu.VMEM((streams - SIDE_FIRST, own, stretch), BF16),
             dma((3,)),
             pltpu.SemaphoreType.REGULAR,
             dma((micro,)),
@@ -447,10 +544,12 @@
             dma,
             dma,
             dma((depth,)),
-            dma((streams,)),
-            dma((streams, depth - 1)),
-            dma,
-            dma((streams,)),
+            dma((streams, 2)),
+            dma((streams, 2, depth // 2)),
+            dma,
+            dma((depth,)),
+            dma,
+            dma((streams - SIDE_FIRST,)),
         ],
         compiler_params=pltpu.CompilerParams(
             collective_id=0, has_side_effects=True, vmem_limit_bytes=56 * 1024 * 1024
@@ -463,7 +562,7 @@
         w_up,
         w_down,
     )
-    return grad_in.reshape(tok_rows, width), *grads
+    return finished(grad_in.reshape(tok_rows, width), *grads)
 
 
 def body(tokens, cotangent, w_gate, w_up, w_down):

time: 179 us -> 168 us (0.939)
  Pallas kernels: 173 us -> 166 us
  local copies, waits for them, and re-layouts: 5.07 us -> 0 us
    pallas_call x1, Pallas kernels: 173 us -> 164 us  [run_pipeline(): pl.pallas_call(functools.partial(pipeline_kernel, sections, micro), out_s...]
    unnamed x10 -> x0, local copies, waits for them, and re-layouts: 5.07 us -> none
    pallas_call x0 -> x1, Pallas kernels: none -> 2.52 us  [finished(): pl.pallas_call(finish_kernel, out_shape=tuple((jax.ShapeDtypeStruct(a.sha...]
where the time goes in v4:
time: 168 us; the launch traced here: 167 us
  Pallas kernels  166 us (99%)
    pallas_call x1, Pallas kernels, run_pipeline(): pl.pallas_call(functools.partial(pipeline_kernel, sections, micro), out_s...  164 us

profile of v4, /device:TPU:8, one launch (start us, length us, event | category | flops | bytes accessed | tf_op | source)
XLA Modules:
  0.0 167.0 jit_solution(14415995832396359212)
XLA Ops:
  0.6 163.8 %pipeline.1 = (bf16[15,32,2048]{2,1,0:T(8,128)(2,1)}, f32[64,512]{1,0:T(8,128)}, f32[64,512]{1,0:T(8,128)}, f32[64,512]{1,0:T(8,128)}) custom-call(bf16[15,32,2048]{2,1,0:T(8,128)(2,1)} %bitcast.13, bf16[15,32,2048]{2,1,0:T(8,128)(2,1)} %bitcast.14, bf16[2048,512]{1,0:T(8,128)(2,1)} %bitcast.10, bf16[2048,512]{1,0:T(8,128)(2,1)} %bitcast.11, ...), custom_call_target="tpu_custom_call" | custom-call | tf_op jit(solution)/shard_map/pipeline/pallas_call | solution.py:503
  164.5 2.5 %finish.1 = (bf16[480,2048]{1,0:T(8,128)(2,1)}, f32[64,512]{1,0:T(8,128)}, f32[64,512]{1,0:T(8,128)}, f32[64,512]{1,0:T(8,128)}) custom-call(bf16[480,2048]{1,0:T(8,128)(2,1)} %bitcast.15, f32[64,512]{1,0:T(8,128)} %get-tuple-element.13.g_in, f32[64,512]{1,0:T(8,128)} %get-tuple-element.14.u_in, f32[64,512]{1,0:T(8,128)} %get-tuple-element.15.d_in), custom_call_target="tpu_custom_call" | custom-call | tf_op jit(solution)/shard_map/finish/pallas_call | solution.py:471

commit v5 on v4

--- a/solution.py
+++ b/solution.py
@@ -119,6 +119,20 @@
 
     for friend in (partner, sibling, *ring_to):
         pl.semaphore_signal(barrier, inc=1, device_id=friend, device_id_type=MESH)
+    block = width // depth
+
+    def turned(src, dst, base):
+        @pl.loop(0, depth)
+        def _(k):
+            at = pl.multiple_of(k * block, block)
+            dst[base : base + units, pl.ds(at, block)] = src[pl.ds(at, block), :].T
+
+    def turn_gate_up():
+        turned(wg, wgu_t, 0)
+        turned(wu, wgu_t, units)
+
+    weights[0].wait()
+    turned(wd, wd_t, 0)
     expected = 4 + jnp.where(place < last, 1, 0) + jnp.where(place > 0, 1, 0)
     pl.semaphore_wait(barrier, expected)
 
@@ -130,20 +144,6 @@
                 cot.at[m], g_in.at[m], c_send, g_recv.at[m], device_id=partner, device_id_type=MESH
             ).start()
 
-    block = width // depth
-
-    def turned(src, dst, base):
-        @pl.loop(0, depth)
-        def _(k):
-            at = pl.multiple_of(k * block, block)
-            dst[base : base + units, pl.ds(at, block)] = src[pl.ds(at, block), :].T
-
-    def turn_gate_up():
-        turned(wg, wgu_t, 0)
-        turned(wu, wgu_t, units)
-
-    weights[0].wait()
-    turned(wd, wd_t, 0)
     weights[1].wait()
     weights[2].wait()
 
@@ -331,7 +331,7 @@
         pltpu.make_async_copy(ref, ref, ring_recv.at[n, way, step]).wait()
 
     def ring_step(step, group):
-        for long in (True, False):
+        for long in (False, True):
             for n in group:
                 for way in range(2):
                     if (n % 2 == way) != long or (step == 0 and not long):

time: 168 us -> 166 us (0.988)
  Pallas kernels: 166 us -> 164 us
    pallas_call x1, Pallas kernels: 164 us -> 162 us  [run_pipeline(): pl.pallas_call(functools.partial(pipeline_kernel, sections, micro), out_s...]
where the time goes in v5:
time: 166 us; the launch traced here: 165 us
  Pallas kernels  164 us (99%)
    pallas_call x1, Pallas kernels, run_pipeline(): pl.pallas_call(functools.partial(pipeline_kernel, sections, micro), out_s...  162 us

profile of v5, /device:TPU:8, one launch (start us, length us, event | category | flops | bytes accessed | tf_op | source)
XLA Modules:
  0.0 164.9 jit_solution(15280614384230001835)
XLA Ops:
  0.6 161.7 %pipeline.1 = (bf16[15,32,2048]{2,1,0:T(8,128)(2,1)}, f32[64,512]{1,0:T(8,128)}, f32[64,512]{1,0:T(8,128)}, f32[64,512]{1,0:T(8,128)}) custom-call(bf16[15,32,2048]{2,1,0:T(8,128)(2,1)} %bitcast.13, bf16[15,32,2048]{2,1,0:T(8,128)(2,1)} %bitcast.14, bf16[2048,512]{1,0:T(8,128)(2,1)} %bitcast.10, bf16[2048,512]{1,0:T(8,128)(2,1)} %bitcast.11, ...), custom_call_target="tpu_custom_call" | custom-call | tf_op jit(solution)/shard_map/pipeline/pallas_call | solution.py:503
  162.4 2.5 %finish.1 = (bf16[480,2048]{1,0:T(8,128)(2,1)}, f32[64,512]{1,0:T(8,128)}, f32[64,512]{1,0:T(8,128)}, f32[64,512]{1,0:T(8,128)}) custom-call(bf16[480,2048]{1,0:T(8,128)(2,1)} %bitcast.15, f32[64,512]{1,0:T(8,128)} %get-tuple-element.13.g_in, f32[64,512]{1,0:T(8,128)} %get-tuple-element.14.u_in, f32[64,512]{1,0:T(8,128)} %get-tuple-element.15.d_in), custom_call_target="tpu_custom_call" | custom-call | tf_op jit(solution)/shard_map/finish/pallas_call | solution.py:471

commit v6 on v5

--- a/solution.py
+++ b/solution.py
@@ -11,8 +11,8 @@
 MICRO = 15
 AHEAD = 4
 CHUNKS = 2
-STREAMS = 4
-SIDE_FIRST = 2
+STREAMS = 6
+SIDE_FIRST = 3
 PIECES = 5
 DP = ("dp_0", "dp_1", "dp_2")
 MESH = pl.DeviceIdType.MESH
@@ -196,6 +196,8 @@
         ) * (1.0 / width)
         shrink = r * inner
         dgu = jnp.concatenate([dg, du], axis=1)
+        dgu_s[m, :, :units] = (d_gate * r).astype(BF16)
+        dgu_s[m, :, units:] = (d_up * r).astype(BF16)
         for k, cols in enumerate(chunks):
             normed_grad = jnp.dot(dgu, wgu_t[:, cols], preferred_element_type=F32)
             g_out[m, :, cols] = (
@@ -228,9 +230,6 @@
         @pl.when(jnp.logical_not(upper))
         def _():
             pltpu.make_async_copy(g_out.at[m], grad_in.at[m], o_recv).start()
-
-        dgu_s[m, :, :units] = (d_gate * r).astype(BF16)
-        dgu_s[m, :, units:] = (d_up * r).astype(BF16)
 
     lead = jnp.minimum(1 + AHEAD * (last - place), micro)
 

time: 166 us -> 166 us (level)
  no operation moved by 1% of the time
where the time goes in v6:
time: 166 us; the launch traced here: 164 us
  Pallas kernels  164 us (99%)
    pallas_call x1, Pallas kernels, run_pipeline(): pl.pallas_call(functools.partial(pipeline_kernel, sections, micro), out_s...  161 us

profile of v6, /device:TPU:8, one launch (start us, length us, event | category | flops | bytes accessed | tf_op | source)
XLA Modules:
  0.0 164.2 jit_solution(18036819915017944732)
XLA Ops:
  0.6 161.1 %pipeline.1 = (bf16[15,32,2048]{2,1,0:T(8,128)(2,1)}, f32[64,512]{1,0:T(8,128)}, f32[64,512]{1,0:T(8,128)}, f32[64,512]{1,0:T(8,128)}) custom-call(bf16[15,32,2048]{2,1,0:T(8,128)(2,1)} %bitcast.13, bf16[15,32,2048]{2,1,0:T(8,128)(2,1)} %bitcast.14, bf16[2048,512]{1,0:T(8,128)(2,1)} %bitcast.10, bf16[2048,512]{1,0:T(8,128)(2,1)} %bitcast.11, ...), custom_call_target="tpu_custom_call" | custom-call | tf_op jit(solution)/shard_map/pipeline/pallas_call | solution.py:502
  161.7 2.5 %finish.1 = (bf16[480,2048]{1,0:T(8,128)(2,1)}, f32[64,512]{1,0:T(8,128)}, f32[64,512]{1,0:T(8,128)}, f32[64,512]{1,0:T(8,128)}) custom-call(bf16[480,2048]{1,0:T(8,128)(2,1)} %bitcast.15, f32[64,512]{1,0:T(8,128)} %get-tuple-element.13.g_in, f32[64,512]{1,0:T(8,128)} %get-tuple-element.14.u_in, f32[64,512]{1,0:T(8,128)} %get-tuple-element.15.d_in), custom_call_target="tpu_custom_call" | custom-call | tf_op jit(solution)/shard_map/finish/pallas_call | solution.py:470
